TPU v7x, 32 devices: a whole 2x2x4 slice. The times are simulated.
32 devices in a mesh: batch: 16 (over z, y, x), tensor: 2 (over core).
Axes of the slice: x: 2, y: 2, z: 4, core: 2. Of those that a mesh axis runs over, the one named last changes fastest.
Arguments:
- tokens: bfloat16 [16, 768, 1152], P('batch'), may hold values from -6 to 6
- segment_ids: int32 [16, 768], P('batch'), may hold values from 0 to 7, never falling along the last dimension, each value on 1 to 256 neighbouring positions
- conditions: bfloat16 [16, 8, 1152], P('batch'), may hold values from -6 to 6
- condition_segment: int32 [16, 8], P('batch'), may hold values from 0 to 7, each once within a row
- qkv_weight: bfloat16 [1152, 3, 1152], P(None, None, 'tensor'), may hold values from -0.1875 to 0.1875
- qv_bias: float32 [2, 1152], P(None, 'tensor'), may hold values from -3 to 3
- proj_weight: bfloat16 [1152, 1152], P('tensor'), may hold values from -0.875 to 0.875
- proj_bias: float32 [1152], replicated, may hold values from -3 to 3
- up_weight: bfloat16 [1152, 4608], P(None, 'tensor'), may hold values from -0.1875 to 0.1875
- up_bias: float32 [4608], P('tensor'), may hold values from -3 to 3
- down_weight: bfloat16 [4608, 1152], P('tensor'), may hold values from -0.09375 to 0.09375
- down_bias: float32 [1152], replicated, may hold values from -3 to 3
- mod_weight: bfloat16 [1152, 6, 1152], P(None, None, 'tensor'), may hold values from -0.1875 to 0.1875
- mod_bias: float32 [6, 1152], P(None, 'tensor'), may hold values from -3 to 3
- out_grad: bfloat16 [16, 768, 1152], P('batch'), may hold values from -6 to 6
Outputs:
- layer_out: bfloat16 [16, 768, 1152], P('batch')
- token_grad: float32 [16, 768, 1152], P('batch', None, 'tensor')
- condition_grad: float32 [16, 8, 1152], P('batch')
- qkv_grad: float32 [1152, 3, 1152], P('batch', None, 'tensor')
- qvbias_grad: float32 [2, 1152], P(None, 'tensor')
- proj_grad: float32 [1152, 1152], P('tensor', 'batch')
- projbias_grad: float32 [1152], replicated
- up_grad: float32 [1152, 4608], P('batch', 'tensor')
- upbias_grad: float32 [4608], P('tensor')
- down_grad: float32 [4608, 1152], P('tensor', 'batch')
- downbias_grad: float32 [1152], replicated
- mod_grad: float32 [1152, 6, 1152], P('batch', None, 'tensor')
- modbias_grad: float32 [6, 1152], P(None, 'tensor')
Inputs may be any that keep to these rules, and one draw needn't show every extreme that they name: `segment_ids`: along each row the ids never fall; each of the 8 segments of a row holds 1 to 256 positions, and some row has a segment of exactly 256 positions. `condition_segment`: each row is a permutation of 0 to 7.
All inputs are finite; a program needn't handle non-finite values.
Results may differ from a plain program's by a relative error of at most 0.022.
The roundings to bfloat16 on the way count: a program that leaves them out, or rounds other values in their place, can miss the bound.
Values may be sent and summed in bfloat16 or wider, within the bound.
No kernel may reach another device: no remote copies, remote signals or barrier semaphores. Data moves between devices by JAX's collectives and lax.ppermute only.
A program may use at most 256 MiB of HBM per device.

v0:
```python
import jax
import jax.numpy as jnp
from jax import lax
from jax.sharding import PartitionSpec as P

HEAD_DIM = 72


EPS = 1e-06
HIGHEST = lax.Precision.HIGHEST


def silu(array):
    return array / (1.0 + jnp.exp(-array))


def gelu(array):
    tanh_arg = 0.7978845608028654 * (array + 0.044715 * array * array * array)
    return 0.5 * array * (1.0 + jnp.tanh(tanh_arg))


def normalize(array):
    center = array - jnp.mean(array, axis=-1, keepdims=True)
    spread = jnp.mean(center * center, axis=-1, keepdims=True)
    inverse = lax.rsqrt(spread + EPS)
    return (center * inverse, inverse)


def segment_pick(one_hot, table):
    return jnp.einsum("rls,rsc->rlc", one_hot, table, precision=HIGHEST)


def segment_total(one_hot, array):
    return jnp.einsum("rls,rlc->rsc", one_hot, array, precision=HIGHEST)


def attention_scores(queries, key_vecs, same_image, score_scale):
    scores = (
        jnp.einsum("rqhe,rkhe->rhqk", queries, key_vecs, preferred_element_type=jnp.float32)
        * score_scale
    )
    return jnp.where(same_image, scores, -1e30)


def on_device(
    tokens,
    segment_ids,
    conditions,
    condition_segment,
    qkv_weight,
    qv_bias,
    proj_weight,
    proj_bias,
    up_weight,
    up_bias,
    down_weight,
    down_bias,
    mod_weight,
    mod_bias,
    out_grad,
):
    row_count = tokens.shape[0]
    length = tokens.shape[1]
    model_width = tokens.shape[2]
    local_width = qkv_weight.shape[2]
    local_heads = local_width // HEAD_DIM
    head_shape = (row_count, length, local_heads, HEAD_DIM)
    score_scale = HEAD_DIM ** (-0.5)
    offset = lax.axis_index("tensor") * local_width

    def mine(array):
        return lax.dynamic_slice_in_dim(array, offset, local_width, 2)

    cond_float = conditions.astype(jnp.float32)
    cond_act = silu(cond_float).astype(jnp.bfloat16)
    mod_local = (
        jnp.einsum("rsd,djc->rsjc", cond_act, mod_weight, preferred_element_type=jnp.float32)
        + mod_bias
    )
    modulation = lax.all_gather(mod_local, "tensor", axis=3, tiled=True)
    one_hot = (segment_ids[:, :, None] == condition_segment[:, None, :]).astype(jnp.float32)
    shift_one = segment_pick(one_hot, modulation[:, :, 0])
    scale_one = segment_pick(one_hot, modulation[:, :, 1])
    gate_one = segment_pick(one_hot, modulation[:, :, 2])
    shift_two = segment_pick(one_hot, modulation[:, :, 3])
    scale_two = segment_pick(one_hot, modulation[:, :, 4])
    gate_two = segment_pick(one_hot, modulation[:, :, 5])
    tok_float = tokens.astype(jnp.float32)
    normed_one, inverse_one = normalize(tok_float)
    attn_in = (normed_one * (1.0 + scale_one) + shift_one).astype(jnp.bfloat16)
    projected = jnp.einsum("rld,djc->rljc", attn_in, qkv_weight, preferred_element_type=jnp.float32)
    queries = (projected[:, :, 0] + qv_bias[0]).astype(jnp.bfloat16).reshape(head_shape)
    key_vecs = projected[:, :, 1].astype(jnp.bfloat16).reshape(head_shape)
    values = (projected[:, :, 2] + qv_bias[1]).astype(jnp.bfloat16).reshape(head_shape)
    same_image = (segment_ids[:, :, None] == segment_ids[:, None, :])[:, None]
    scores = attention_scores(queries, key_vecs, same_image, score_scale)
    row_peak = jnp.max(scores, axis=-1, keepdims=True)
    shifted = jnp.exp(scores - row_peak)
    row_total = jnp.sum(shifted, axis=-1, keepdims=True)
    attn_probs = shifted / row_total
    log_total = row_peak + jnp.log(row_total)
    attended = jnp.einsum(
        "rhqk,rkhe->rqhe",
        attn_probs.astype(jnp.bfloat16),
        values,
        preferred_element_type=jnp.float32,
    )
    attended = attended.astype(jnp.bfloat16).reshape(row_count, length, local_width)
    proj_part = jnp.einsum("rlc,cd->rld", attended, proj_weight, preferred_element_type=jnp.float32)
    attn_out = lax.psum(proj_part.astype(jnp.bfloat16), "tensor").astype(jnp.float32) + proj_bias
    middle = tok_float + gate_one * attn_out
    normed_two, inverse_two = normalize(middle)
    mlp_in = (normed_two * (1.0 + scale_two) + shift_two).astype(jnp.bfloat16)
    hidden = (
        jnp.einsum("rld,df->rlf", mlp_in, up_weight, preferred_element_type=jnp.float32) + up_bias
    )
    active = gelu(hidden).astype(jnp.bfloat16)
    down_part = jnp.einsum("rlf,fd->rld", active, down_weight, preferred_element_type=jnp.float32)
    mlp_out = lax.psum(down_part.astype(jnp.bfloat16), "tensor").astype(jnp.float32) + down_bias
    layer_out = (middle + gate_two * mlp_out).astype(jnp.bfloat16)
    grad_float = out_grad.astype(jnp.float32)
    mlp_grad = (grad_float * gate_two).astype(jnp.bfloat16)
    gate_two_grad = grad_float * mlp_out
    down_bias_grad = jnp.sum(mlp_grad.astype(jnp.float32), axis=(0, 1))
    down_weight_grad = jnp.einsum(
        "rlf,rld->fd", active, mlp_grad, preferred_element_type=jnp.float32
    )
    active_grad = jnp.einsum(
        "rld,fd->rlf", mlp_grad, down_weight, preferred_element_type=jnp.float32
    )
    gelu_pull = jax.vjp(gelu, hidden)[1]
    hidden_grad = gelu_pull(active_grad)[0].astype(jnp.bfloat16)
    up_bias_grad = jnp.sum(hidden_grad.astype(jnp.float32), axis=(0, 1))
    up_weight_grad = jnp.einsum(
        "rld,rlf->df", mlp_in, hidden_grad, preferred_element_type=jnp.float32
    )
    mlp_part = jnp.einsum("rlf,df->rld", hidden_grad, up_weight, preferred_element_type=jnp.float32)
    mlp_in_grad = lax.psum(mlp_part.astype(jnp.bfloat16), "tensor").astype(jnp.float32)
    scale_two_grad = mlp_in_grad * normed_two
    scaled_two = mlp_in_grad * (1.0 + scale_two)
    middle_grad = grad_float + inverse_two * (
        scaled_two
        - jnp.mean(scaled_two, axis=-1, keepdims=True)
        - normed_two * jnp.mean(scaled_two * normed_two, axis=-1, keepdims=True)
    )
    attn_grad = (middle_grad * gate_one).astype(jnp.bfloat16)
    gate_one_grad = middle_grad * attn_out
    mlp_in_share = mine(mlp_in_grad)
    scale_two_share = mine(scale_two_grad)
    middle_share = mine(middle_grad)
    gate_one_share = mine(gate_one_grad)
    proj_bias_grad = jnp.sum(attn_grad.astype(jnp.float32), axis=(0, 1))
    proj_weight_grad = jnp.einsum(
        "rlc,rld->cd", attended, attn_grad, preferred_element_type=jnp.float32
    )
    attended_grad = jnp.einsum(
        "rld,cd->rlc", attn_grad, proj_weight, preferred_element_type=jnp.float32
    )
    attended_grad = attended_grad.astype(jnp.bfloat16).reshape(head_shape)
    scores = attention_scores(queries, key_vecs, same_image, score_scale)
    attn_probs = jnp.exp(scores - log_total)
    value_grad = jnp.einsum(
        "rhqk,rqhe->rkhe",
        attn_probs.astype(jnp.bfloat16),
        attended_grad,
        preferred_element_type=jnp.float32,
    )
    prob_grad = jnp.einsum(
        "rqhe,rkhe->rhqk", attended_grad, values, preferred_element_type=jnp.float32
    )
    score_grad = attn_probs * (prob_grad - jnp.sum(prob_grad * attn_probs, axis=-1, keepdims=True))
    score_grad = score_grad.astype(jnp.bfloat16)
    query_grad = (
        jnp.einsum("rhqk,rkhe->rqhe", score_grad, key_vecs, preferred_element_type=jnp.float32)
        * score_scale
    )
    key_grad = (
        jnp.einsum("rhqk,rqhe->rkhe", score_grad, queries, preferred_element_type=jnp.float32)
        * score_scale
    )
    flat_shape = (row_count, length, local_width)
    triple_grad = jnp.stack(
        [
            query_grad.reshape(flat_shape),
            key_grad.reshape(flat_shape),
            value_grad.reshape(flat_shape),
        ],
        axis=2,
    ).astype(jnp.bfloat16)
    qv_bias_grad = jnp.sum(triple_grad[:, :, 0::2].astype(jnp.float32), axis=(0, 1))
    qkv_weight_grad = jnp.einsum(
        "rld,rljc->djc", attn_in, triple_grad, preferred_element_type=jnp.float32
    )
    attn_part = jnp.einsum(
        "rljc,djc->rld", triple_grad, qkv_weight, preferred_element_type=jnp.float32
    )
    attn_in_grad = lax.psum_scatter(
        attn_part.astype(jnp.bfloat16), "tensor", scatter_dimension=2, tiled=True
    ).astype(jnp.float32)
    normed_mine = mine(normed_one)
    scaled_one = attn_in_grad * (1.0 + mine(scale_one))
    row_sums = jnp.sum(scaled_one, axis=-1)
    cross_sums = jnp.sum(scaled_one * normed_mine, axis=-1)
    token_parts = (
        attn_in_grad,
        attn_in_grad * normed_mine,
        gate_one_share,
        mlp_in_share,
        scale_two_share,
        mine(gate_two_grad),
    )
    mod_tgrad = jnp.stack([segment_total(one_hot, part) for part in token_parts], axis=2).astype(
        jnp.bfloat16
    )
    mod_bias_grad = jnp.sum(mod_tgrad.astype(jnp.float32), axis=(0, 1))
    mod_weight_grad = jnp.einsum(
        "rsd,rsjc->djc", cond_act, mod_tgrad, preferred_element_type=jnp.float32
    )
    cond_part = jnp.einsum(
        "rsjc,djc->rsd", mod_tgrad, mod_weight, preferred_element_type=jnp.float32
    )
    row_whole, cross_whole, cond_act_grad = (
        lax.psum(row_sums.astype(jnp.bfloat16), "tensor").astype(jnp.float32),
        lax.psum(cross_sums.astype(jnp.bfloat16), "tensor").astype(jnp.float32),
        lax.psum(cond_part.astype(jnp.bfloat16), "tensor").astype(jnp.float32),
    )
    token_grad = middle_share + inverse_one * (
        scaled_one
        - row_whole[:, :, None] / model_width
        - normed_mine * (cross_whole[:, :, None] / model_width)
    )
    silu_pull = jax.vjp(silu, cond_float)[1]
    condition_grad = silu_pull(cond_act_grad)[0]
    qkv_sum, proj_sum, up_sum, down_sum, mod_sum = (
        lax.psum_scatter(
            qkv_weight_grad.astype(jnp.bfloat16), "batch", scatter_dimension=0, tiled=True
        ).astype(jnp.float32),
        lax.psum_scatter(
            proj_weight_grad.astype(jnp.bfloat16), "batch", scatter_dimension=1, tiled=True
        ).astype(jnp.float32),
        lax.psum_scatter(
            up_weight_grad.astype(jnp.bfloat16), "batch", scatter_dimension=0, tiled=True
        ).astype(jnp.float32),
        lax.psum_scatter(
            down_weight_grad.astype(jnp.bfloat16), "batch", scatter_dimension=1, tiled=True
        ).astype(jnp.float32),
        lax.psum_scatter(
            mod_weight_grad.astype(jnp.bfloat16), "batch", scatter_dimension=0, tiled=True
        ).astype(jnp.float32),
    )
    qv_sum, projbias_sum, upbias_sum, downbias_sum, modbias_sum = lax.psum(
        (qv_bias_grad, proj_bias_grad, up_bias_grad, down_bias_grad, mod_bias_grad), "batch"
    )
    return (
        layer_out,
        token_grad,
        condition_grad,
        qkv_sum,
        qv_sum,
        proj_sum,
        projbias_sum,
        up_sum,
        upbias_sum,
        down_sum,
        downbias_sum,
        mod_sum,
        modbias_sum,
    )


def solution(mesh):
    return jax.shard_map(
        on_device,
        mesh=mesh,
        in_specs=(
            P("batch", None, None),
            P("batch", None),
            P("batch", None, None),
            P("batch", None),
            P(None, None, "tensor"),
            P(None, "tensor"),
            P("tensor", None),
            P(),
            P(None, "tensor"),
            P("tensor"),
            P("tensor", None),
            P(),
            P(None, None, "tensor"),
            P(None, "tensor"),
            P("batch", None, None),
        ),
        out_specs=(
            P("batch", None, None),
            P("batch", None, "tensor"),
            P("batch", None, None),
            P("batch", None, "tensor"),
            P(None, "tensor"),
            P("tensor", "batch"),
            P(),
            P("batch", "tensor"),
            P("tensor"),
            P("tensor", "batch"),
            P(),
            P("batch", None, "tensor"),
            P(None, "tensor"),
        ),
        check_vma=False,
    )
```

profile of v0, /device:TPU:0, one launch (start us, length us, event | category | flops | bytes accessed | tf_op | source)
XLA Modules:
  0.0 1112.6 jit_solution(12797852679350489927)
XLA Ops:
  12.5 5.6 convolution_add_fusion.1
  20.3 24.0 %all-gather = f32[8,6,1152]{1,0,2:T(8,128)} all-gather(f32[8,6,576]{1,0,2:T(8,128)} %copy.47), channel_id=2, replica_groups=mesh['batch'=16,'tensor'=2] {'tensor'}, dimensions={2}, use_global_device_ids=true | all-gather | bytes 331776 | tf_op jit(solution)/shard_map/all_gather | solution.py:80
  44.3 3.7 copy.48
  54.1 3.6 convolution_bitcast_fusion.5
  61.0 11.8 %fusion.152 = (f32[8,768]{1,0:T(8,128)S(1)}, f32[8,768,768]{1,2,0:T(8,128)}) fusion(bf16[768,8,72]{0,2,1:T(8,128)(2,1)} %bitcast.286, f32[768,8,72]{0,2,1:T(8,128)} %bitcast.283, f32[8,72]{1,0:T(8,128)S(1)} %add.199, pred[768,768]{0,1:T(8,128)(4,1)} %broadcast_compare_fusion), kind=kOutput, calls=%fused_computation.230 | convolution fusion | flops 694511616 | bytes 22145280 | tf_op jit(solution)/shard_map/rqhe,rkhe->rhqk/dot_general | solution.py:39
  72.8 9.3 fusion
  82.0 10.4 fusion.55
  96.4 3.4 fusion.16
  99.7 4.8 convert_reduce_fusion.2
  104.6 15.0 %all-reduce.9.cloned.1.call-done = bf16[1,768,1152]{2,1,0:T(8,128)(2,1)} async-done(((bf16[1,768,1152]{2,1,0:T(8,128)(2,1)}), bf16[1,768,1152]{2,1,0:T(8,128)(2,1)}) %all-reduce.9.cloned.1.call-update) | async-done | bytes 1769488 | tf_op jit(solution)/shard_map/psum | solution.py:110
  119.6 8.2 fusion.150
  134.5 7.4 fusion.153
  141.9 7.6 fusion.23
  149.5 10.0 convert_reduce_fusion
  161.4 5.9 fusion.24
  167.4 25.3 %all-reduce.13.cloned.1.call-done = (bf16[1,768,1152]{2,1,0:T(8,128)(2,1)}, bf16[1,768,1152]{2,1,0:T(8,128)(2,1)}) async-done(((bf16[1,768,1152]{2,1,0:T(8,128)(2,1)}, bf16[1,768,1152]{2,1,0:T(8,128)(2,1)}), (bf16[1,768,1152]{2,1,0:T(8,128)(2,1)}, bf16[1,768,1152]{2,1,0:T(8,128)(2,1)})) %all-reduce.13.cloned.1.call-update) | async-done | bytes 3538960 | tf_op jit(solution)/shard_map/psum | solution.py:119
  192.7 4.8 fusion.77
  198.8 4.9 convert_reduce_fusion.3
  205.1 9.5 fusion.56
  214.7 12.4 %multiply_reduce_fusion = (f32[8,768]{1,0:T(8,128)S(1)}, f32[8,768,768]{1,2,0:T(8,128)}) fusion(f32[8,768,768]{1,2,0:T(8,128)} %get-tuple-element.95, f32[8,768]{1,0:T(8,128)S(1)} %log_add_fusion, bf16[768,8,72]{0,2,1:T(8,128)(2,1)S(1)} %bitcast.295, f32[768,8,72]{0,2,1:T(8,128)S(1)} %bitcast.289, f32[8,72]{1,0:T(8,128)S(1)} %add.196), kind=kOutput, calls=%fused_computation.1 | convolution fusion | flops 694511616 | bytes 40454400 | tf_op jit(solution)/shard_map/rqhe,rkhe->rhqk/dot_general | solution.py:168
  227.1 12.9 %multiply_convert_fusion = bf16[8,768,768]{1,2,0:T(8,128)(2,1)S(1)} fusion(f32[8,768,768]{1,2,0:T(8,128)} %get-tuple-element.99, f32[8,768,768]{1,2,0:T(8,128)} %get-tuple-element.95, f32[8,768]{1,0:T(8,128)S(1)} %get-tuple-element.98, f32[8,768]{1,0:T(8,128)S(1)} %log_add_fusion), kind=kLoop, calls=%fused_computation | loop fusion | flops 18874368 | bytes 47235072 | tf_op jit(solution)/shard_map/convert_element_type | solution.py:172
  245.8 5.0 fusion.28
  250.9 9.2 copy.61
  260.1 3.6 copy.70
  263.7 4.2 convolution_convert_fusion.7
  268.0 11.0 convolution_convert_fusion.1
  279.1 9.3 convolution_convert_fusion.2
  289.6 5.8 convolution_convert_fusion.3
  295.4 18.2 %copy.63 = bf16[1152,3,576]{2,1,0:T(4,128)(2,1)} copy(bf16[1152,3,576]{2,0,1:T(8,128)(2,1)S(1)} %convolution_convert_fusion.3) | data formatting | bytes 7962624
  313.7 12.3 %reshape.1053 = bf16[1152,1728]{1,0:T(8,128)(2,1)} reshape(bf16[1152,3,576]{2,1,0:T(4,128)(2,1)} %copy.63) | data formatting | bytes 7962624
  326.0 3.5 convert_element_type.262
  332.8 5.6 convert_add_fusion.1
  338.4 3.3 reshape_bitcast_fusion
  341.7 3.9 copy.62
  348.7 3.4 constant_dynamic-update-slice_fusion.3
  352.5 3.2 constant_dynamic-update-slice_fusion.1
  355.7 3.2 constant_dynamic-update-slice_fusion
  358.9 6.0 convolution_convert_fusion
  368.6 30.2 %reduce-scatter.21.cloned.1.call-done = bf16[576,72]{0,1:T(8,128)(2,1)} async-done(((bf16[576,1152]{0,1:T(8,128)(2,1)}), bf16[576,72]{0,1:T(8,128)(2,1)}) %reduce-scatter.21.cloned.1.call-update) | async-done | bytes 82960
  400.3 3.8 fusion.79
  404.1 4.4 fusion.30
  408.5 3.7 all-reduce.3
  412.3 5.2 multiply_add_fusion.2
  419.3 76.6 %all-reduce.2 = (f32[2,576]{1,0:T(2,128)}, f32[1152]{0:T(1024)}, f32[2304]{0:T(1024)}, f32[1152]{0:T(1024)}, f32[6,576]{1,0:T(8,128)}) all-reduce(f32[2,576]{1,0:T(2,128)S(1)} %convert_reduce_fusion.4, f32[1152]{0:T(1024)S(1)} %get-tuple-element.83, ...), channel_id=1, replica_groups=mesh['batch'=16,'tensor'=2] {'batch'}, use_global_device_ids=true, to_apply=%region_20.21 | all-reduce | flops 9216 | bytes 73728 | tf_op jit(solution)/shard_map/psum | solution.py:251
  496.6 47.0 %reduce-scatter.15.cloned.1.call-done = bf16[2304,72]{0,1:T(8,128)(2,1)} async-done(((bf16[2304,1152]{0,1:T(8,128)(2,1)}), bf16[2304,72]{0,1:T(8,128)(2,1)}) %reduce-scatter.15.cloned.1.call-update) | async-done | bytes 331792 | tf_op jit(solution)/shard_map/reduce_scatter | solution.py:244
  545.4 143.4 %reduce-scatter.13.cloned.1.call-done = bf16[72,2304]{1,0:T(8,128)(2,1)} async-done(((bf16[1152,2304]{1,0:T(8,128)(2,1)}), bf16[72,2304]{1,0:T(8,128)(2,1)}) %reduce-scatter.13.cloned.1.call-update) | async-done | bytes 331792 | tf_op jit(solution)/shard_map/reduce_scatter | solution.py:241
  690.6 139.0 %reduce-scatter.19.cloned.1.call-done = bf16[72,1728]{1,0:T(8,128)(2,1)} async-done(((bf16[1152,1728]{1,0:T(8,128)(2,1)}), bf16[72,1728]{1,0:T(8,128)(2,1)}) %reduce-scatter.19.cloned.1.call-update) | async-done | bytes 248848
  831.6 271.7 %all-reduce.11.cloned.1.call-done = bf16[1152,6,576]{2,0,1:T(8,128)(2,1)} async-done(((bf16[1152,6,576]{2,0,1:T(8,128)(2,1)}), bf16[1152,6,576]{2,0,1:T(8,128)(2,1)}) %all-reduce.11.cloned.1.call-update) | async-done | bytes 7962640
  (172 shorter events, 60.9 us)
Async XLA Ops:
  7.2 86.2 %copy-start = (bf16[576,1152]{1,0:T(8,128)(2,1)S(1)}, bf16[576,1152]{1,0:T(8,128)(2,1)}, u32[]{:S(2)}) copy-start(bf16[576,1152]{1,0:T(8,128)(2,1)} %param.21) | copy-start | bytes 3981316
  7.2 4.0 copy-start.38
  7.2 5.3 copy-start.28
  7.2 5.3 copy-start.34
  7.2 112.3 %all-reduce.9.cloned.1.call-start = ((), (), s32[]{:S(2)}) async-start(), calls=%async_computation.5 | async-start | bytes 3538944 | tf_op jit(solution)/shard_map/psum | solution.py:110
  11.3 108.3 %copy-start.31 = (f32[768]{0:T(1024)}, f32[768]{0:T(1024)S(1)}, u32[]{:S(2)}) copy-start(f32[768]{0:T(1024)S(1)} %add_rsqrt_fusion.1) | copy-start | bytes 9220
  44.3 3.7 copy-start.30
  44.3 7.3 copy-start.7
  49.7 1.9 copy-start.6
  51.6 2.4 copy-start.39
  54.1 3.7 copy-start.25
  58.8 2.0 copy-start.37
  96.3 96.4 %all-reduce.13.cloned.1.call-start = ((), (), s32[]{:S(2)}) async-start(), calls=%async_computation.12 | async-start | bytes 7077888 | tf_op jit(solution)/shard_map/psum | solution.py:119
  96.3 3.4 copy-start.11
  99.7 19.8 %copy-start.35 = (f32[1152]{0:T(1024)S(1)}, f32[1152]{0:T(1024)}, u32[]{:S(2)}) copy-start(f32[1152]{0:T(1024)} %param.22) | copy-start | bytes 13828
  128.3 2.7 copy-start.4
  131.0 2.1 copy-start.8
  131.0 10.8 slice-start
  134.4 7.4 slice-start.1
  134.5 7.4 copy-start.41
  141.8 7.6 copy-start.45
  141.9 7.6 copy-start.26
  141.9 19.5 %slice-start.2 = ((s8[5308416]{0:T(1024)(128)(4,1)}), s8[4194304]{0:T(1024)(128)(4,1)S(1)}, s32[]{:S(2)}) async-start(s8[5308416]{0:T(1024)(128)(4,1)} %bitcast.322), calls=%async_computation.15 | async-start | bytes 8388608
  149.5 11.9 %slice-start.3 = ((s8[5308416]{0:T(1024)(128)(4,1)}), s8[1114112]{0:T(1024)(128)(4,1)S(1)}, s32[]{:S(2)}) async-start(s8[5308416]{0:T(1024)(128)(4,1)} %bitcast.322), calls=%async_computation.16 | async-start | bytes 2228224
  167.3 171.1 %reduce-scatter.17.cloned.1.call-start = ((), (), s32[]{:S(2)}) async-start(), calls=%async_computation.8 | async-start | bytes 2654208
  192.6 4.8 copy-start.3
  192.7 5.7 copy-start.5
  192.7 6.1 copy-start.10
  205.1 9.6 copy-start.17
  214.7 30.2 %copy-start.21 = (bf16[8,72,768]{2,1,0:T(8,128)(2,1)}, bf16[8,72,768]{2,1,0:T(8,128)(2,1)S(1)}, u32[]{:S(2)}) copy-start(bf16[8,72,768]{2,1,0:T(8,128)(2,1)S(1)} %fusion.56) | copy-start | bytes 2654212
  227.1 12.9 %copy-start.12 = (f32[1,768,1,576]{1,3,2,0:T(8,128)S(1)}, f32[1,768,1,576]{1,3,2,0:T(8,128)}, u32[]{:S(2)}) copy-start(f32[1,768,1,576]{1,3,2,0:T(8,128)} %get-tuple-element.89) | copy-start | bytes 5308420
  240.0 3.0 copy-start.15
  243.1 2.8 copy-start.40
  260.1 3.7 copy-start.43
  263.7 135.1 %reduce-scatter.21.cloned.1.call-start = ((), (), s32[]{:S(2)}) async-start(), calls=%async_computation.11 | async-start | bytes 1566720
  268.0 275.6 %reduce-scatter.15.cloned.1.call-start = ((), (), s32[]{:S(2)}) async-start(), calls=%async_computation.7 | async-start | bytes 5640192 | tf_op jit(solution)/shard_map/reduce_scatter | solution.py:244
  279.1 409.7 %reduce-scatter.13.cloned.1.call-start = ((), (), s32[]{:S(2)}) async-start(), calls=%async_computation.6 | async-start | bytes 5640192 | tf_op jit(solution)/shard_map/reduce_scatter | solution.py:241
  288.4 541.2 %reduce-scatter.19.cloned.1.call-start = ((), (), s32[]{:S(2)}) async-start(), calls=%async_computation.9 | async-start | bytes 4386816
  326.0 777.4 %all-reduce.11.cloned.1.call-start = ((), (), s32[]{:S(2)}) async-start(), calls=%async_computation.10 | async-start | bytes 17694720
  329.5 2.0 copy-start.36
  329.5 3.3 copy-start.14
  345.5 3.1 copy-start.13
  345.8 6.7 copy-start.9
  348.7 7.1 copy-start.16
  352.5 6.4 copy-start.29
  364.9 1.9 copy-start.22
  404.1 8.1 copy-start.32
  417.5 688.0 %copy-start.1 = (bf16[576,1152]{1,0:T(8,128)(2,1)S(1)}, bf16[576,1152]{1,0:T(8,128)(2,1)}, u32[]{:S(2)}) copy-start(bf16[576,1152]{1,0:T(8,128)(2,1)} %param.21) | copy-start | bytes 3981316
  (11 other events, 15.6 us)
Sparse Core Ops, SparseCore 0:
  96.4 23.1 all-reduce.8
  167.4 25.1 all-reduce.12
  263.8 10.4 reduce-scatter.16
  279.8 118.9 reduce-scatter.20
  403.9 139.6 reduce-scatter.14
  548.7 140.0 reduce-scatter.12
  693.9 135.6 reduce-scatter.18
  835.8 267.4 all-reduce.10
where the time goes:
time: 1120 us; the launch traced here: 1110 us
  waiting for transfers between devices  672 us (60%)
  matrix products  175 us (16%)
  blocking collectives  104 us (9%)
  local copies, waits for them, and re-layouts  76.6 us (7%)
  other arithmetic  68.8 us (6%)
  between operations  15.7 us (1%)
    unnamed x12, waiting for transfers between devices  441 us
    reduce_scatter x1, waiting for transfers between devices, on_device(): lax.psum_scatter(up_weight_grad.astype(jnp.bfloat16), 'batch', scatter_di...  143 us
    psum x1, blocking collectives, on_device(): lax.psum((qv_bias_grad, proj_bias_grad, up_bias_grad, down_bias_grad, mod...  76.6 us
    unnamed x116, local copies, waits for them, and re-layouts  67.5 us
    reduce_scatter x1, waiting for transfers between devices, on_device(): lax.psum_scatter(down_weight_grad.astype(jnp.bfloat16), 'batch', scatter_...  47 us
    psum x1, waiting for transfers between devices, on_device(): lax.psum(down_part.astype(jnp.bfloat16), 'tensor').astype(jnp.float32)  25.3 us
    all_gather x1, blocking collectives, on_device(): modulation = lax.all_gather(mod_local, 'tensor', axis=3, tiled=True)  24 us
    dot_general x6, matrix products, segment_pick(): return jnp.einsum('rls,rsc->rlc', one_hot, table, precision=HIGHEST)  22.6 us
  transfers between devices with their start and end apart: 8, of which 7 were waited for; matrix products, arithmetic and copies ran while one was open for 12% of the time, Pallas kernels for 0%

commit v1 on v0

--- a/solution.py
+++ b/solution.py
@@ -1,3 +1,5 @@
+import functools
+
 import jax
 import jax.numpy as jnp
 from jax import lax
@@ -34,6 +36,71 @@
     return jnp.einsum("rls,rlc->rsc", one_hot, array, precision=HIGHEST)
 
 
+def exchange(array, axis):
+    return lax.ppermute(array, axis, [(0, 1), (1, 0)])
+
+
+def tensor_sum(array, size):
+    if size == 2:
+        return array.astype(jnp.float32) + exchange(array, "tensor").astype(jnp.float32)
+    return lax.psum(array, "tensor").astype(jnp.float32)
+
+
+def tensor_join(array, size):
+    if size == 2:
+        other = exchange(array, "tensor")
+        first = lax.axis_index("tensor") == 0
+        return jnp.concatenate(
+            [jnp.where(first, array, other), jnp.where(first, other, array)], axis=-1
+        )
+    return lax.all_gather(array, "tensor", axis=array.ndim - 1, tiled=True)
+
+
+def partners(size, bit):
+    return [(i, i ^ (1 << bit)) for i in range(size)]
+
+
+def batch_gather(array, size):
+    out = array[None]
+    for bit in range(size.bit_length() - 1):
+        other = lax.ppermute(out, "batch", partners(size, bit))
+        out = jnp.concatenate([out, other], axis=0)
+    return out
+
+
+def batch_scatter(part, size, order):
+    bits = size.bit_length() - 1
+    index = lax.axis_index("batch")
+    cube = part.reshape((2,) * bits + part.shape[1:])
+    for step, bit in enumerate(order):
+        axis = bits - 1 - bit
+        mine = (index >> bit) & 1
+        send = lax.dynamic_index_in_dim(cube, 1 - mine, axis, keepdims=True)
+        keep = lax.dynamic_index_in_dim(cube, mine, axis, keepdims=True)
+        got = lax.ppermute(send, "batch", partners(size, bit))
+        cube = keep.astype(jnp.float32) + got.astype(jnp.float32)
+        if step < bits - 1:
+            cube = cube.astype(jnp.bfloat16)
+    return cube.reshape(part.shape[1:])
+
+
+def weight_grad(left, right, size):
+    bits = size.bit_length() - 1
+    depth = right.shape[-1]
+    cut = depth // 256 * 128
+    orders = (tuple(range(bits)), (1, 0) + tuple(range(2, bits)))
+    pieces = []
+    for begin, end, order in ((0, cut, orders[0]), (cut, depth, orders[1])):
+        if begin == end:
+            continue
+        part = jnp.einsum(
+            "rld,rlc->dc", left, right[:, :, begin:end], preferred_element_type=jnp.float32
+        ).astype(jnp.bfloat16)
+        part = part.reshape((size, part.shape[0] // size, part.shape[1]))
+        pieces.append(batch_scatter(part, size, order))
+    return jnp.concatenate(pieces, axis=1)
+
+
 def attention_scores(queries, key_vecs, same_image, score_scale):
     scores = (
         jnp.einsum("rqhe,rkhe->rhqk", queries, key_vecs, preferred_element_type=jnp.float32)
@@ -43,6 +110,7 @@
 
 
 def on_device(
+    n_batch,
     tokens,
     segment_ids,
     conditions,
@@ -67,6 +135,7 @@
     head_shape = (row_count, length, local_heads, HEAD_DIM)
     score_scale = HEAD_DIM ** (-0.5)
     offset = lax.axis_index("tensor") * local_width
+    n_tensor = model_width // local_width
 
     def mine(array):
         return lax.dynamic_slice_in_dim(array, offset, local_width, 2)
@@ -77,7 +146,7 @@
         jnp.einsum("rsd,djc->rsjc", cond_act, mod_weight, preferred_element_type=jnp.float32)
         + mod_bias
     )
-    modulation = lax.all_gather(mod_local, "tensor", axis=3, tiled=True)
+    modulation = tensor_join(mod_local, n_tensor)
     one_hot = (segment_ids[:, :, None] == condition_segment[:, None, :]).astype(jnp.float32)
     shift_one = segment_pick(one_hot, modulation[:, :, 0])
     scale_one = segment_pick(one_hot, modulation[:, :, 1])
@@ -107,7 +176,7 @@
     )
     attended = attended.astype(jnp.bfloat16).reshape(row_count, length, local_width)
     proj_part = jnp.einsum("rlc,cd->rld", attended, proj_weight, preferred_element_type=jnp.float32)
-    attn_out = lax.psum(proj_part.astype(jnp.bfloat16), "tensor").astype(jnp.float32) + proj_bias
+    attn_out = tensor_sum(proj_part.astype(jnp.bfloat16), n_tensor) + proj_bias
     middle = tok_float + gate_one * attn_out
     normed_two, inverse_two = normalize(middle)
     mlp_in = (normed_two * (1.0 + scale_two) + shift_two).astype(jnp.bfloat16)
@@ -116,26 +185,22 @@
     )
     active = gelu(hidden).astype(jnp.bfloat16)
     down_part = jnp.einsum("rlf,fd->rld", active, down_weight, preferred_element_type=jnp.float32)
-    mlp_out = lax.psum(down_part.astype(jnp.bfloat16), "tensor").astype(jnp.float32) + down_bias
+    mlp_out = tensor_sum(down_part.astype(jnp.bfloat16), n_tensor) + down_bias
     layer_out = (middle + gate_two * mlp_out).astype(jnp.bfloat16)
     grad_float = out_grad.astype(jnp.float32)
     mlp_grad = (grad_float * gate_two).astype(jnp.bfloat16)
     gate_two_grad = grad_float * mlp_out
     down_bias_grad = jnp.sum(mlp_grad.astype(jnp.float32), axis=(0, 1))
-    down_weight_grad = jnp.einsum(
-        "rlf,rld->fd", active, mlp_grad, preferred_element_type=jnp.float32
-    )
+    down_sum = weight_grad(mlp_grad, active, n_batch).T
     active_grad = jnp.einsum(
         "rld,fd->rlf", mlp_grad, down_weight, preferred_element_type=jnp.float32
     )
     gelu_pull = jax.vjp(gelu, hidden)[1]
     hidden_grad = gelu_pull(active_grad)[0].astype(jnp.bfloat16)
     up_bias_grad = jnp.sum(hidden_grad.astype(jnp.float32), axis=(0, 1))
-    up_weight_grad = jnp.einsum(
-        "rld,rlf->df", mlp_in, hidden_grad, preferred_element_type=jnp.float32
-    )
+    up_sum = weight_grad(mlp_in, hidden_grad, n_batch)
     mlp_part = jnp.einsum("rlf,df->rld", hidden_grad, up_weight, preferred_element_type=jnp.float32)
-    mlp_in_grad = lax.psum(mlp_part.astype(jnp.bfloat16), "tensor").astype(jnp.float32)
+    mlp_in_grad = tensor_sum(mlp_part.astype(jnp.bfloat16), n_tensor)
     scale_two_grad = mlp_in_grad * normed_two
     scaled_two = mlp_in_grad * (1.0 + scale_two)
     middle_grad = grad_float + inverse_two * (
@@ -150,9 +215,7 @@
     middle_share = mine(middle_grad)
     gate_one_share = mine(gate_one_grad)
     proj_bias_grad = jnp.sum(attn_grad.astype(jnp.float32), axis=(0, 1))
-    proj_weight_grad = jnp.einsum(
-        "rlc,rld->cd", attended, attn_grad, preferred_element_type=jnp.float32
-    )
+    proj_sum = weight_grad(attn_grad, attended, n_batch).T
     attended_grad = jnp.einsum(
         "rld,cd->rlc", attn_grad, proj_weight, preferred_element_type=jnp.float32
     )
@@ -188,15 +251,20 @@
         axis=2,
     ).astype(jnp.bfloat16)
     qv_bias_grad = jnp.sum(triple_grad[:, :, 0::2].astype(jnp.float32), axis=(0, 1))
-    qkv_weight_grad = jnp.einsum(
-        "rld,rljc->djc", attn_in, triple_grad, preferred_element_type=jnp.float32
-    )
+    flat_triple = triple_grad.reshape((row_count, length, 3 * local_width))
+    qkv_sum = weight_grad(attn_in, flat_triple, n_batch).reshape((-1, 3, local_width))
     attn_part = jnp.einsum(
         "rljc,djc->rld", triple_grad, qkv_weight, preferred_element_type=jnp.float32
     )
-    attn_in_grad = lax.psum_scatter(
-        attn_part.astype(jnp.bfloat16), "tensor", scatter_dimension=2, tiled=True
-    ).astype(jnp.float32)
+    attn_part = attn_part.astype(jnp.bfloat16)
+    if n_tensor == 2:
+        kept = mine(attn_part)
+        sent = lax.dynamic_slice_in_dim(attn_part, local_width - offset, local_width, 2)
+        attn_in_grad = kept.astype(jnp.float32) + exchange(sent, "tensor").astype(jnp.float32)
+    else:
+        attn_in_grad = lax.psum_scatter(
+            attn_part, "tensor", scatter_dimension=2, tiled=True
+        ).astype(jnp.float32)
     normed_mine = mine(normed_one)
     scaled_one = attn_in_grad * (1.0 + mine(scale_one))
     row_sums = jnp.sum(scaled_one, axis=-1)
@@ -212,17 +280,23 @@
     mod_tgrad = jnp.stack([segment_total(one_hot, part) for part in token_parts], axis=2).astype(
         jnp.bfloat16
     )
-    mod_bias_grad = jnp.sum(mod_tgrad.astype(jnp.float32), axis=(0, 1))
-    mod_weight_grad = jnp.einsum(
-        "rsd,rsjc->djc", cond_act, mod_tgrad, preferred_element_type=jnp.float32
-    )
+    cond_all = batch_gather(cond_act, n_batch)
+    tgrad_all = batch_gather(mod_tgrad, n_batch)
+    block = model_width // n_batch
+    cond_block = lax.dynamic_slice_in_dim(
+        cond_all, lax.axis_index("batch") * block, block, cond_all.ndim - 1
+    )
+    mod_sum = jnp.einsum(
+        "prsd,prsjc->djc", cond_block, tgrad_all, preferred_element_type=jnp.float32
+    )
+    modbias_sum = jnp.sum(tgrad_all.astype(jnp.float32), axis=(0, 1, 2))
     cond_part = jnp.einsum(
         "rsjc,djc->rsd", mod_tgrad, mod_weight, preferred_element_type=jnp.float32
     )
     row_whole, cross_whole, cond_act_grad = (
-        lax.psum(row_sums.astype(jnp.bfloat16), "tensor").astype(jnp.float32),
-        lax.psum(cross_sums.astype(jnp.bfloat16), "tensor").astype(jnp.float32),
-        lax.psum(cond_part.astype(jnp.bfloat16), "tensor").astype(jnp.float32),
+        tensor_sum(row_sums.astype(jnp.bfloat16), n_tensor),
+        tensor_sum(cross_sums.astype(jnp.bfloat16), n_tensor),
+        tensor_sum(cond_part.astype(jnp.bfloat16), n_tensor),
     )
     token_grad = middle_share + inverse_one * (
         scaled_one
@@ -231,26 +305,17 @@
     )
     silu_pull = jax.vjp(silu, cond_float)[1]
     condition_grad = silu_pull(cond_act_grad)[0]
-    qkv_sum, proj_sum, up_sum, down_sum, mod_sum = (
-        lax.psum_scatter(
-            qkv_weight_grad.astype(jnp.bfloat16), "batch", scatter_dimension=0, tiled=True
-        ).astype(jnp.float32),
-        lax.psum_scatter(
-            proj_weight_grad.astype(jnp.bfloat16), "batch", scatter_dimension=1, tiled=True
-        ).astype(jnp.float32),
-        lax.psum_scatter(
-            up_weight_grad.astype(jnp.bfloat16), "batch", scatter_dimension=0, tiled=True
-        ).astype(jnp.float32),
-        lax.psum_scatter(
-            down_weight_grad.astype(jnp.bfloat16), "batch", scatter_dimension=1, tiled=True
-        ).astype(jnp.float32),
-        lax.psum_scatter(
-            mod_weight_grad.astype(jnp.bfloat16), "batch", scatter_dimension=0, tiled=True
-        ).astype(jnp.float32),
-    )
-    qv_sum, projbias_sum, upbias_sum, downbias_sum, modbias_sum = lax.psum(
-        (qv_bias_grad, proj_bias_grad, up_bias_grad, down_bias_grad, mod_bias_grad), "batch"
-    )
+    widths = (2 * local_width, model_width, up_bias.shape[0], model_width)
+    flat_bias = jnp.concatenate(
+        [qv_bias_grad.reshape(-1), proj_bias_grad, up_bias_grad, down_bias_grad]
+    )
+    flat_bias = jnp.sum(batch_gather(flat_bias, n_batch), axis=0)
+    pieces = []
+    for width in widths:
+        pieces.append(flat_bias[:width])
+        flat_bias = flat_bias[width:]
+    qv_sum, projbias_sum, upbias_sum, downbias_sum = pieces
+    qv_sum = qv_sum.reshape((2, local_width))
     return (
         layer_out,
         token_grad,
@@ -270,7 +335,7 @@
 
 def solution(mesh):
     return jax.shard_map(
-        on_device,
+        functools.partial(on_device, mesh.shape["batch"]),
         mesh=mesh,
         in_specs=(
             P("batch", None, None),

time: 1120 us -> 507 us (0.45)
  waiting for transfers between devices: 672 us -> 143 us
  blocking collectives: 104 us -> 0 us
  starting transfers between devices: 0.5 us -> 50 us
  local copies, waits for them, and re-layouts: 76.6 us -> 58.5 us
  other arithmetic: 68.8 us -> 84.5 us
  matrix products: 175 us -> 160 us
  between operations: 15.7 us -> 2.56 us
    unnamed x12 -> x0, waiting for transfers between devices: 441 us -> none
    reduce_scatter x2 -> x0, waiting for transfers between devices: 190 us -> none  [the longest x1 143 us: on_device(): lax.psum_scatter(up_weight_grad.astype(jnp.bfloat16), 'batch', scatter_di...]
    ppermute x0 -> x52, waiting for transfers between devices: none -> 143 us  [the longest x32 129 us: batch_scatter(): got = lax.ppermute(send, 'batch', partners(size, bit))]
    psum x2 -> x0, blocking collectives: 80.3 us -> none  [the longest x1 76.6 us: on_device(): lax.psum((qv_bias_grad, proj_bias_grad, up_bias_grad, down_bias_grad, mod...]
    unnamed x116 -> x151, local copies, waits for them, and re-layouts: 67.5 us -> 17.3 us
    ppermute x0 -> x52, starting transfers between devices: none -> 50 us  [the longest x32 34.6 us: batch_scatter(): got = lax.ppermute(send, 'batch', partners(size, bit))]
    psum x2 -> x0, waiting for transfers between devices: 40.3 us -> none  [the longest x1 25.3 us: on_device(): lax.psum(down_part.astype(jnp.bfloat16), 'tensor').astype(jnp.float32)]
    all_gather x1 -> x0, blocking collectives: 24 us -> none  [on_device(): modulation = lax.all_gather(mod_local, 'tensor', axis=3, tiled=True)]
  transfers between devices with their start and end apart: 8 -> 52, of which waited for: 7 -> 21; matrix products, arithmetic and copies ran while one was open for 12% -> 39% of each run, Pallas kernels for 0% -> 0%
where the time goes in v1:
time: 507 us; the launch traced here: 498 us
  matrix products  160 us (32%)
  waiting for transfers between devices  143 us (28%)
  other arithmetic  84.5 us (17%)
  local copies, waits for them, and re-layouts  58.5 us (12%)
  starting transfers between devices  50 us (10%)
    ppermute x32, waiting for transfers between devices, batch_scatter(): got = lax.ppermute(send, 'batch', partners(size, bit))  129 us
    ppermute x32, starting transfers between devices, batch_scatter(): got = lax.ppermute(send, 'batch', partners(size, bit))  34.6 us
    dot_general x6, matrix products, segment_pick(): return jnp.einsum('rls,rsc->rlc', one_hot, table, precision=HIGHEST)  20.3 us
    dot_general x8, matrix products, weight_grad(): jnp.einsum('rld,rlc->dc', left, right[:, :, begin:end], preferred_element...  20.1 us
    convert_element_type x24, other arithmetic, batch_scatter(): cube = cube.astype(jnp.bfloat16)  18.5 us
    dot_general x6, matrix products, segment_total(): return jnp.einsum('rls,rlc->rsc', one_hot, array, precision=HIGHEST)  18.4 us
    unnamed x151, local copies, waits for them, and re-layouts  17.3 us
    dynamic_slice x32, local copies, waits for them, and re-layouts, batch_scatter(): send = lax.dynamic_index_in_dim(cube, 1 - mine, axis, keepdims=True)  15.1 us
  transfers between devices with their start and end apart: 52, of which 21 were waited for; matrix products, arithmetic and copies ran while one was open for 39% of the time, Pallas kernels for 0%

profile of v1, /device:TPU:0, one launch (start us, length us, event | category | flops | bytes accessed | tf_op | source)
XLA Modules:
  0.0 498.3 jit_solution(2144097983046739685)
XLA Ops:
  0.7 5.7 %fusion.72 = f32[1,8,6,576]{3,1,2,0:T(8,128)S(1)} fusion(bf16[1152,6,576]{0,2,1:T(8,128)(2,1)} %param.27, f32[6,576]{1,0:T(8,128)} %param.28, bf16[1,8,1152]{2,1,0:T(8,128)(2,1)} %param.17), kind=kOutput, calls=%fused_computation.148 | convolution fusion | flops 63774720 | bytes 8105472 | tf_op jit(solution)/shard_map/rsd,djc->rsjc/dot_general | solution.py:146
  16.2 3.7 convolution_bitcast_fusion.5
  21.5 8.6 %fusion.202 = (f32[8,768]{1,0:T(8,128)S(1)}, f32[8,768,768]{1,2,0:T(8,128)}) fusion(bf16[768,8,72]{0,2,1:T(8,128)(2,1)S(1)} %bitcast.398, f32[768,8,72]{0,2,1:T(8,128)S(1)} %bitcast.394, f32[8,72]{1,0:T(8,128)S(1)} %add.396, pred[768,768]{0,1:T(8,128)(4,1)S(1)} %copy-done.30), kind=kOutput, calls=%fused_computation.398 | convolution fusion | flops 694511616 | bytes 22145280 | tf_op jit(solution)/shard_map/rqhe,rkhe->rhqk/dot_general | solution.py:106
  30.1 8.9 %fusion = f32[8,768]{1,0:T(8,128)S(1)} fusion(f32[8,768,768]{1,2,0:T(8,128)} %get-tuple-element.114, f32[8,768]{1,0:T(8,128)S(1)} %get-tuple-element.113), kind=kLoop, calls=%fused_computation.6 | loop fusion | flops 9431040 | bytes 18923520 | tf_op jit(solution)/shard_map/reduce_sum | solution.py:168
  39.0 10.4 %fusion.68 = bf16[8,72,768]{2,1,0:T(8,128)(2,1)S(1)} fusion(f32[8,768,768]{1,2,0:T(8,128)} %get-tuple-element.114, f32[8,768]{1,0:T(8,128)S(1)} %fusion, f32[8,768]{1,0:T(8,128)S(1)} %get-tuple-element.113, f32[768,8,72]{0,2,1:T(8,128)} %bitcast.402, f32[8,72]{1,0:T(8,128)S(1)} %add.393), kind=kOutput, calls=%fused_computation.137 | convolution fusion | flops 694960128 | bytes 21580032 | tf_op jit(solution)/shard_map/rhqk,rkhe->rqhe/dot_general | solution.py:171
  49.4 2.9 fusion.25
  52.4 3.4 convert_element_type.599
  57.5 6.8 %fusion.199 = (f32[768]{0:T(1024)S(1)}, f32[1,768,1152]{2,1,0:T(8,128)S(1)}, f32[1,768,1152]{2,1,0:T(8,128)}, f32[1,768,1152]{2,1,0:T(8,128)}, f32[1,768,1152]{2,1,0:T(8,128)S(1)}) fusion(bf16[1,768,1152]{2,1,0:T(8,128)(2,1)S(1)} %copy-done.3, f32[1152]{0:T(1024)S(1)} %copy-done.51, bf16[1,768,1152]{2,1,0:T(8,128)(2,1)} %collective-permute-done.1, ...), kind=kOutput, calls=%fused_computation.395 | convolution fusion | flops 93796608 | bytes 19702304 | tf_op jit(solution)/shard_map/rls,rsc->rlc/dot_general | solution.py:32
  69.1 4.7 fusion.203
  73.9 6.3 %fusion.23 = bf16[1,768,1152]{2,1,0:T(8,128)(2,1)S(1)} fusion(bf16[2304,1152]{1,0:T(8,128)(2,1)S(1)} %bitcast.439, f32[768,2304]{1,0:T(8,128)S(1)} %fusion.203, f32[2304]{0:T(1024)S(1)} %copy-done.49), kind=kOutput, calls=%fused_computation.66 | convolution fusion | flops 4095442944 | bytes 14164992 | tf_op jit(solution)/shard_map/rlf,fd->rld/dot_general | solution.py:187
  84.0 5.7 %convert_reduce_fusion.2 = (f32[1152]{0:T(1024)}, bf16[1,768,1152]{2,1,0:T(8,128)(2,1)S(1)}, bf16[1,768,1152]{2,1,0:T(8,128)(2,1)}, f32[1,768,1152]{2,1,0:T(8,128)}) fusion(bf16[1,768,1152]{2,1,0:T(8,128)(2,1)S(1)} %copy-done.9, f32[1,768,1152]{2,1,0:T(8,128)S(1)} %get-tuple-element.79, f32[1152]{0:T(1024)S(1)} %copy-done.52, ...), kind=kOutput, calls=%fused_computation.46 | convolution fusion | flops 95565696 | bytes 16158752 | tf_op jit(solution)/shard_map/rls,rsc->rlc/dot_general | solution.py:32
  89.8 13.1 %convert_reduce_fusion = (f32[2304]{0:T(1024)}, bf16[768,2304]{1,0:T(8,128)(2,1)}) fusion(f32[768,2304]{1,0:T(8,128)S(1)} %fusion.203, f32[2304]{0:T(1024)S(1)} %copy-done.49, bf16[2304,1152]{1,0:T(8,128)(2,1)} %param.25, bf16[1,768,1152]{2,1,0:T(8,128)(2,1)S(1)} %get-tuple-element.75), kind=kOutput, calls=%fused_computation.25 | convolution fusion | flops 4124636928 | bytes 17713152 | tf_op jit(solution)/shard_map/rld,fd->rlf/dot_general | solution.py:195
  102.9 8.5 %fusion.24 = bf16[1,768,1152]{2,1,0:T(8,128)(2,1)S(1)} fusion(bf16[768,2304]{1,0:T(8,128)(2,1)} %get-tuple-element.131, bf16[1152,2304]{1,0:T(8,128)(2,1)} %param.23), kind=kOutput, calls=%fused_computation.67 | convolution fusion | flops 4077748224 | bytes 10616832 | tf_op jit(solution)/shard_map/rlf,df->rld/dot_general | solution.py:202
  117.0 2.7 collective-permute-start.28
  123.9 3.0 convolution_convert_fusion.1
  127.8 21.9 %collective-permute-done.28 = bf16[2,2,2,1,72,1152]{5,4,3,2,1,0:T(8,128)(2,1)} collective-permute-done((bf16[2,2,2,1,72,1152]{5,4,3,2,1,0:T(8,128)(2,1)S(1)}, bf16[2,2,2,1,72,1152]{5,4,3,2,1,0:T(8,128)(2,1)}, u32[]{:S(2)}, u32[]{:S(2)}) %collective-permute-start.28) | collective-permute-done | bytes 1327136 | tf_op jit(solution)/shard_map/ppermute | solution.py:80
  158.5 19.5 %collective-permute-done.36 = bf16[2,2,2,1,72,1152]{5,4,3,2,1,0:T(8,128)(2,1)S(1)} collective-permute-done((bf16[2,2,2,1,72,1152]{5,4,3,2,1,0:T(8,128)(2,1)S(1)}, bf16[2,2,2,1,72,1152]{5,4,3,2,1,0:T(8,128)(2,1)S(1)}, u32[]{:S(2)}, u32[]{:S(2)}) %collective-permute-start.36) | collective-permute-done | bytes 1327136 | tf_op jit(solution)/shard_map/ppermute | solution.py:80
  185.7 3.8 convert_reduce_fusion.3
  194.1 9.5 %fusion.3 = bf16[8,72,768]{2,1,0:T(8,128)(2,1)S(1)} fusion(bf16[768,8,72]{0,2,1:T(8,128)(2,1)S(1)} %bitcast.406, f32[8,768,768]{1,2,0:T(8,128)} %get-tuple-element.114, f32[8,768]{1,0:T(8,128)S(1)} %log_add_fusion), kind=kOutput, calls=%fused_computation.12 | convolution fusion | flops 688914432 | bytes 20668416 | tf_op jit(solution)/shard_map/rhqk,rqhe->rkhe/dot_general | solution.py:225
  203.6 12.4 %multiply_reduce_fusion = (f32[8,768]{1,0:T(8,128)S(1)}, f32[8,768,768]{1,2,0:T(8,128)}) fusion(f32[8,768,768]{1,2,0:T(8,128)} %get-tuple-element.114, f32[8,768]{1,0:T(8,128)S(1)} %log_add_fusion, bf16[768,8,72]{0,2,1:T(8,128)(2,1)S(1)} %bitcast.407, f32[768,8,72]{0,2,1:T(8,128)S(1)} %bitcast.403, f32[8,72]{1,0:T(8,128)S(1)} %add.393), kind=kOutput, calls=%fused_computation.1 | convolution fusion | flops 694511616 | bytes 40454400 | tf_op jit(solution)/shard_map/rqhe,rkhe->rhqk/dot_general | solution.py:231
  216.0 13.4 %multiply_convert_fusion = bf16[8,768,768]{1,2,0:T(8,128)(2,1)S(1)} fusion(f32[8,768,768]{1,2,0:T(8,128)} %get-tuple-element.117, f32[8,768,768]{1,2,0:T(8,128)} %get-tuple-element.114, f32[8,768]{1,0:T(8,128)S(1)} %get-tuple-element.116, f32[8,768]{1,0:T(8,128)S(1)} %log_add_fusion), kind=kLoop, calls=%fused_computation | loop fusion | flops 18874368 | bytes 47235072 | tf_op jit(solution)/shard_map/convert_element_type | solution.py:235
  229.4 3.0 convolution_multiply_fusion
  235.7 2.8 convolution_convert_fusion.6
  238.5 3.5 convolution_convert_fusion.4
  245.9 4.4 copy.63
  252.7 6.6 %fusion.20 = bf16[768,1152]{1,0:T(8,128)(2,1)S(1)} fusion(bf16[1152,3,576]{0,2,1:T(8,128)(2,1)} %param.19, bf16[768,1,576]{0,2,1:T(8,128)(2,1)} %bitcast.411, bf16[768,1,576]{0,2,1:T(8,128)(2,1)} %bitcast.413, bf16[768,1,576]{0,2,1:T(8,128)(2,1)S(1)} %bitcast.405), kind=kOutput, calls=%fused_computation.58 | convolution fusion | flops 3061186560 | bytes 8404992 | tf_op jit(solution)/shard_map/rljc,djc->rld/dot_general | solution.py:256
  303.1 6.3 %collective-permute-done.19 = f32[8,5760]{1,0:T(8,128)} collective-permute-done((f32[8,5760]{1,0:T(8,128)S(1)}, f32[8,5760]{1,0:T(8,128)}, u32[]{:S(2)}, u32[]{:S(2)}) %collective-permute-start.19) | collective-permute-done | bytes 184352 | tf_op jit(solution)/shard_map/ppermute | solution.py:66
  320.6 5.6 %collective-permute-done.21 = bf16[2,2,1,1,72,256]{5,4,3,2,1,0:T(8,128)(2,1)S(1)} collective-permute-done((bf16[2,2,1,1,72,256]{5,4,3,2,1,0:T(8,128)(2,1)}, bf16[2,2,1,1,72,256]{5,4,3,2,1,0:T(8,128)(2,1)S(1)}, u32[]{:S(2)}, u32[]{:S(2)}) %collective-permute-start.21) | collective-permute-done | bytes 147488 | tf_op jit(solution)/shard_map/ppermute | solution.py:80
  327.7 3.9 collective-permute-done.22
  334.8 7.7 %collective-permute-done.34 = bf16[2,1,1,1,72,1152]{5,4,3,2,1,0:T(8,128)(2,1)S(1)} collective-permute-done((bf16[2,1,1,1,72,1152]{5,4,3,2,1,0:T(8,128)(2,1)}, bf16[2,1,1,1,72,1152]{5,4,3,2,1,0:T(8,128)(2,1)S(1)}, u32[]{:S(2)}, u32[]{:S(2)}) %collective-permute-start.34) | collective-permute-done | bytes 331808 | tf_op jit(solution)/shard_map/ppermute | solution.py:80
  343.1 6.6 %collective-permute-done.38 = bf16[2,1,1,1,72,1152]{5,4,3,2,1,0:T(8,128)(2,1)S(1)} collective-permute-done((bf16[2,1,1,1,72,1152]{5,4,3,2,1,0:T(8,128)(2,1)S(1)}, bf16[2,1,1,1,72,1152]{5,4,3,2,1,0:T(8,128)(2,1)S(1)}, u32[]{:S(2)}, u32[]{:S(2)}) %collective-permute-start.38) | collective-permute-done | bytes 331808 | tf_op jit(solution)/shard_map/ppermute | solution.py:80
  354.0 3.0 collective-permute-start.23
  357.4 5.5 %collective-permute-done.26 = bf16[2,1,1,1,72,320]{5,4,3,2,1,0:T(8,128)(2,1)S(1)} collective-permute-done((bf16[2,1,1,1,72,320]{5,4,3,2,1,0:T(8,128)(2,1)S(1)}, bf16[2,1,1,1,72,320]{5,4,3,2,1,0:T(8,128)(2,1)S(1)}, u32[]{:S(2)}, u32[]{:S(2)}) %collective-permute-start.26) | collective-permute-done | bytes 92192 | tf_op jit(solution)/shard_map/ppermute | solution.py:80
  365.9 11.9 %collective-permute-done.27 = bf16[1,1,1,1,72,320]{5,4,3,2,1,0:T(8,128)(2,1)S(1)} collective-permute-done((bf16[1,1,1,1,72,320]{5,4,3,2,1,0:T(8,128)(2,1)S(1)}, bf16[1,1,1,1,72,320]{5,4,3,2,1,0:T(8,128)(2,1)S(1)}, u32[]{:S(2)}, u32[]{:S(2)}) %collective-permute-start.27) | collective-permute-done | bytes 46112 | tf_op jit(solution)/shard_map/ppermute | solution.py:80
  378.6 2.9 collective-permute-start.39
  381.5 6.8 %collective-permute-done.35 = bf16[1,1,1,1,72,1152]{5,4,3,2,1,0:T(8,128)(2,1)S(1)} collective-permute-done((bf16[1,1,1,1,72,1152]{5,4,3,2,1,0:T(8,128)(2,1)S(1)}, bf16[1,1,1,1,72,1152]{5,4,3,2,1,0:T(8,128)(2,1)S(1)}, u32[]{:S(2)}, u32[]{:S(2)}) %collective-permute-start.35) | collective-permute-done | bytes 165920 | tf_op jit(solution)/shard_map/ppermute | solution.py:80
  391.0 4.6 collective-permute-done.43
  401.5 4.6 fusion.196
  406.8 3.0 constant_dynamic-update-slice_fusion.4
  409.8 3.3 constant_dynamic-update-slice_fusion.3
  415.7 3.2 constant_dynamic-update-slice_fusion.1
  418.9 3.8 constant_dynamic-update-slice_fusion
  433.2 4.2 multiply_add_fusion.2
  437.4 2.8 copy.66
  445.6 3.7 collective-permute-done.46
  461.5 5.8 %collective-permute-done.10 = bf16[2,1,1,1,72,768]{5,4,3,2,1,0:T(8,128)(2,1)S(1)} collective-permute-done((bf16[2,1,1,1,72,768]{5,4,3,2,1,0:T(8,128)(2,1)S(1)}, bf16[2,1,1,1,72,768]{5,4,3,2,1,0:T(8,128)(2,1)S(1)}, u32[]{:S(2)}, u32[]{:S(2)}) %collective-permute-start.10) | collective-permute-done | bytes 221216 | tf_op jit(solution)/shard_map/ppermute | solution.py:80
  469.7 17.8 %collective-permute-done.11 = bf16[1,1,1,1,72,768]{5,4,3,2,1,0:T(8,128)(2,1)S(1)} collective-permute-done((bf16[1,1,1,1,72,768]{5,4,3,2,1,0:T(8,128)(2,1)S(1)}, bf16[1,1,1,1,72,768]{5,4,3,2,1,0:T(8,128)(2,1)S(1)}, u32[]{:S(2)}, u32[]{:S(2)}) %collective-permute-start.11) | collective-permute-done | bytes 110624 | tf_op jit(solution)/shard_map/ppermute | solution.py:80
  490.1 6.4 %collective-permute-done.15 = bf16[1,1,1,1,72,960]{5,4,3,2,1,0:T(8,128)(2,1)S(1)} collective-permute-done((bf16[1,1,1,1,72,960]{5,4,3,2,1,0:T(8,128)(2,1)S(1)}, bf16[1,1,1,1,72,960]{5,4,3,2,1,0:T(8,128)(2,1)S(1)}, u32[]{:S(2)}, u32[]{:S(2)}) %collective-permute-start.15) | collective-permute-done | bytes 138272 | tf_op jit(solution)/shard_map/ppermute | solution.py:80
  (385 shorter events, 177.1 us)
Async XLA Ops:
  52.3 5.2 %collective-permute-start.1 = (bf16[1,768,1152]{2,1,0:T(8,128)(2,1)}, bf16[1,768,1152]{2,1,0:T(8,128)(2,1)}, u32[]{:S(2)}, u32[]{:S(2)}) collective-permute-start(bf16[1,768,1152]{2,1,0:T(8,128)(2,1)} %fusion.25), channel_id=1, source_target_pairs={{0,1},{1,0},{2,3},{3,2},{4,5},{5,4},{6,7},{7,6},{8,9},{9,8},{10,11... | collective-permute-start | bytes 5308424 | tf_op jit(solution)/shard_map/ppermute | solution.py:40
  116.5 67.8 %collective-permute-start.3 = (bf16[1,768,1152]{2,1,0:T(8,128)(2,1)S(1)}, bf16[1,768,1152]{2,1,0:T(8,128)(2,1)S(1)}, u32[]{:S(2)}, u32[]{:S(2)}) collective-permute-start(bf16[1,768,1152]{2,1,0:T(8,128)(2,1)S(1)} %fusion.24), channel_id=1, source_target_pairs={{0,1},{1,0},{2,3},{3,2},{4,5},{5,4},{6,7},{7,6},{8,9},{9,8},{10,11... | collective-permute-start | bytes 5308424 | tf_op jit(solution)/shard_map/ppermute | solution.py:40
  117.0 32.7 %collective-permute-start.28 = (bf16[2,2,2,1,72,1152]{5,4,3,2,1,0:T(8,128)(2,1)S(1)}, bf16[2,2,2,1,72,1152]{5,4,3,2,1,0:T(8,128)(2,1)}, u32[]{:S(2)}, u32[]{:S(2)}) collective-permute-start(bf16[2,2,2,1,72,1152]{5,4,3,2,1,0:T(8,128)(2,1)S(1)} %constant_dynamic-slice_fusion.15), channel_id=1, source_target_pairs={{0,2},{2,0},{4,6},{6,4},{8,10},{10,8},{12,14},{14,12},{16,18},{18,... | collective-permute-start | bytes 3981320 | tf_op jit(solution)/shard_map/ppermute | solution.py:80
  119.8 34.6 %collective-permute-start.32 = (bf16[2,2,1,2,72,1152]{5,4,3,2,1,0:T(8,128)(2,1)S(1)}, bf16[2,2,1,2,72,1152]{5,4,3,2,1,0:T(8,128)(2,1)}, u32[]{:S(2)}, u32[]{:S(2)}) collective-permute-start(bf16[2,2,1,2,72,1152]{5,4,3,2,1,0:T(8,128)(2,1)S(1)} %constant_dynamic-slice_fusion.11), channel_id=1, source_target_pairs={{0,4},{2,6},{4,0},{6,2},{8,12},{10,14},{12,8},{14,10},{16,20},{18,... | collective-permute-start | bytes 3981320 | tf_op jit(solution)/shard_map/ppermute | solution.py:80
  127.0 51.0 %collective-permute-start.36 = (bf16[2,2,2,1,72,1152]{5,4,3,2,1,0:T(8,128)(2,1)S(1)}, bf16[2,2,2,1,72,1152]{5,4,3,2,1,0:T(8,128)(2,1)S(1)}, u32[]{:S(2)}, u32[]{:S(2)}) collective-permute-start(bf16[2,2,2,1,72,1152]{5,4,3,2,1,0:T(8,128)(2,1)S(1)} %constant_dynamic-slice_fusion.7), channel_id=1, source_target_pairs={{0,2},{2,0},{4,6},{6,4},{8,10},{10,8},{12,14},{14,12},{16,18},{18,... | collective-permute-start | bytes 3981320 | tf_op jit(solution)/shard_map/ppermute | solution.py:80
  127.7 53.8 %collective-permute-start.40 = (bf16[2,2,1,2,72,1152]{5,4,3,2,1,0:T(8,128)(2,1)S(1)}, bf16[2,2,1,2,72,1152]{5,4,3,2,1,0:T(8,128)(2,1)S(1)}, u32[]{:S(2)}, u32[]{:S(2)}) collective-permute-start(bf16[2,2,1,2,72,1152]{5,4,3,2,1,0:T(8,128)(2,1)S(1)} %constant_dynamic-slice_fusion.3), channel_id=1, source_target_pairs={{0,4},{2,6},{4,0},{6,2},{8,12},{10,14},{12,8},{14,10},{16,20},{18,... | collective-permute-start | bytes 3981320 | tf_op jit(solution)/shard_map/ppermute | solution.py:80
  152.3 134.8 %collective-permute-start.29 = (bf16[2,2,1,1,72,1152]{5,4,3,2,1,0:T(8,128)(2,1)}, bf16[2,2,1,1,72,1152]{5,4,3,2,1,0:T(8,128)(2,1)}, u32[]{:S(2)}, u32[]{:S(2)}) collective-permute-start(bf16[2,2,1,1,72,1152]{5,4,3,2,1,0:T(8,128)(2,1)} %constant_dynamic-slice_fusion.14), channel_id=1, source_target_pairs={{0,4},{2,6},{4,0},{6,2},{8,12},{10,14},{12,8},{14,10},{16,20},{18,... | collective-permute-start | bytes 1990664 | tf_op jit(solution)/shard_map/ppermute | solution.py:80
  157.0 133.7 %collective-permute-start.33 = (bf16[2,2,1,1,72,1152]{5,4,3,2,1,0:T(8,128)(2,1)}, bf16[2,2,1,1,72,1152]{5,4,3,2,1,0:T(8,128)(2,1)}, u32[]{:S(2)}, u32[]{:S(2)}) collective-permute-start(bf16[2,2,1,1,72,1152]{5,4,3,2,1,0:T(8,128)(2,1)} %constant_dynamic-slice_fusion.10), channel_id=1, source_target_pairs={{0,2},{2,0},{4,6},{6,4},{8,10},{10,8},{12,14},{14,12},{16,18},{18,... | collective-permute-start | bytes 1990664 | tf_op jit(solution)/shard_map/ppermute | solution.py:80
  179.4 113.5 %collective-permute-start.37 = (bf16[2,2,1,1,72,1152]{5,4,3,2,1,0:T(8,128)(2,1)}, bf16[2,2,1,1,72,1152]{5,4,3,2,1,0:T(8,128)(2,1)}, u32[]{:S(2)}, u32[]{:S(2)}) collective-permute-start(bf16[2,2,1,1,72,1152]{5,4,3,2,1,0:T(8,128)(2,1)} %constant_dynamic-slice_fusion.6), channel_id=1, source_target_pairs={{0,4},{2,6},{4,0},{6,2},{8,12},{10,14},{12,8},{14,10},{16,20},{18,... | collective-permute-start | bytes 1990664 | tf_op jit(solution)/shard_map/ppermute | solution.py:80
  182.8 111.9 %collective-permute-start.41 = (bf16[2,2,1,1,72,1152]{5,4,3,2,1,0:T(8,128)(2,1)}, bf16[2,2,1,1,72,1152]{5,4,3,2,1,0:T(8,128)(2,1)}, u32[]{:S(2)}, u32[]{:S(2)}) collective-permute-start(bf16[2,2,1,1,72,1152]{5,4,3,2,1,0:T(8,128)(2,1)} %constant_dynamic-slice_fusion.2), channel_id=1, source_target_pairs={{0,2},{2,0},{4,6},{6,4},{8,10},{10,8},{12,14},{14,12},{16,18},{18,... | collective-permute-start | bytes 1990664 | tf_op jit(solution)/shard_map/ppermute | solution.py:80
  245.3 19.2 %collective-permute-start.16 = (f32[1,5760]{1,0:T(1,128)}, f32[1,5760]{1,0:T(1,128)}, u32[]{:S(2)}, u32[]{:S(2)}) collective-permute-start(f32[1,5760]{1,0:T(1,128)} %broadcast_in_dim.22), channel_id=1, source_target_pairs={{0,2},{2,0},{4,6},{6,4},{8,10},{10,8},{12,14},{14,12},{16,18},{18,... | collective-permute-start | bytes 69128 | tf_op jit(solution)/shard_map/ppermute | solution.py:66
  266.0 4.8 collective-permute-start.17
  272.3 9.1 %collective-permute-start.18 = (f32[4,5760]{1,0:T(4,128)}, f32[4,5760]{1,0:T(4,128)}, u32[]{:S(2)}, u32[]{:S(2)}) collective-permute-start(f32[4,5760]{1,0:T(4,128)} %pad_maximum_fusion.7), channel_id=1, source_target_pairs={{0,8},{2,10},{4,12},{6,14},{8,0},{10,2},{12,4},{14,6},{16,24},{18,... | collective-permute-start | bytes 276488 | tf_op jit(solution)/shard_map/ppermute | solution.py:66
  281.4 16.6 %collective-permute-start.20 = (bf16[2,2,2,1,72,256]{5,4,3,2,1,0:T(8,128)(2,1)}, bf16[2,2,2,1,72,256]{5,4,3,2,1,0:T(8,128)(2,1)}, u32[]{:S(2)}, u32[]{:S(2)}) collective-permute-start(bf16[2,2,2,1,72,256]{5,4,3,2,1,0:T(8,128)(2,1)} %constant_dynamic-slice_fusion.23), channel_id=1, source_target_pairs={{0,2},{2,0},{4,6},{6,4},{8,10},{10,8},{12,14},{14,12},{16,18},{18,... | collective-permute-start | bytes 884744 | tf_op jit(solution)/shard_map/ppermute | solution.py:80
  287.1 30.9 %collective-permute-start.24 = (bf16[2,2,1,2,72,320]{5,4,3,2,1,0:T(8,128)(2,1)}, bf16[2,2,1,2,72,320]{5,4,3,2,1,0:T(8,128)(2,1)}, u32[]{:S(2)}, u32[]{:S(2)}) collective-permute-start(bf16[2,2,1,2,72,320]{5,4,3,2,1,0:T(8,128)(2,1)} %constant_dynamic-slice_fusion.19), channel_id=1, source_target_pairs={{0,4},{2,6},{4,0},{6,2},{8,12},{10,14},{12,8},{14,10},{16,20},{18,... | collective-permute-start | bytes 1105928 | tf_op jit(solution)/shard_map/ppermute | solution.py:80
  290.7 105.9 %collective-permute-start.4 = (bf16[1,768,576]{1,2,0:T(8,128)(2,1)}, bf16[1,768,576]{1,2,0:T(8,128)(2,1)}, u32[]{:S(2)}, u32[]{:S(2)}) collective-permute-start(bf16[1,768,576]{1,2,0:T(8,128)(2,1)} %bitcast.44), channel_id=1, source_target_pairs={{0,1},{1,0},{2,3},{3,2},{4,5},{5,4},{6,7},{7,6},{8,9},{9,8},{10,11... | collective-permute-start | bytes 2654216 | tf_op jit(solution)/shard_map/ppermute | solution.py:40
  292.8 134.9 %collective-permute-start.8 = (bf16[2,2,2,1,72,768]{5,4,3,2,1,0:T(8,128)(2,1)}, bf16[2,2,2,1,72,768]{5,4,3,2,1,0:T(8,128)(2,1)}, u32[]{:S(2)}, u32[]{:S(2)}) collective-permute-start(bf16[2,2,2,1,72,768]{5,4,3,2,1,0:T(8,128)(2,1)} %constant_dynamic-slice_fusion.31), channel_id=1, source_target_pairs={{0,2},{2,0},{4,6},{6,4},{8,10},{10,8},{12,14},{14,12},{16,18},{18,... | collective-permute-start | bytes 2654216 | tf_op jit(solution)/shard_map/ppermute | solution.py:80
  294.7 158.2 %collective-permute-start.12 = (bf16[2,2,1,2,72,960]{5,4,3,2,1,0:T(8,128)(2,1)}, bf16[2,2,1,2,72,960]{5,4,3,2,1,0:T(8,128)(2,1)}, u32[]{:S(2)}, u32[]{:S(2)}) collective-permute-start(bf16[2,2,1,2,72,960]{5,4,3,2,1,0:T(8,128)(2,1)} %constant_dynamic-slice_fusion.27), channel_id=1, source_target_pairs={{0,4},{2,6},{4,0},{6,2},{8,12},{10,14},{12,8},{14,10},{16,20},{18,... | collective-permute-start | bytes 3317768 | tf_op jit(solution)/shard_map/ppermute | solution.py:80
  298.1 11.3 %collective-permute-start.19 = (f32[8,5760]{1,0:T(8,128)S(1)}, f32[8,5760]{1,0:T(8,128)}, u32[]{:S(2)}, u32[]{:S(2)}) collective-permute-start(f32[8,5760]{1,0:T(8,128)S(1)} %pad_maximum_fusion.4), channel_id=1, source_target_pairs={{0,16},{2,18},{4,20},{6,22},{8,24},{10,26},{12,28},{14,30},{16,0},... | collective-permute-start | bytes 552968 | tf_op jit(solution)/shard_map/ppermute | solution.py:66
  309.3 22.8 %collective-permute-start.30 = (bf16[2,1,1,1,72,1152]{5,4,3,2,1,0:T(8,128)(2,1)}, bf16[2,1,1,1,72,1152]{5,4,3,2,1,0:T(8,128)(2,1)}, u32[]{:S(2)}, u32[]{:S(2)}) collective-permute-start(bf16[2,1,1,1,72,1152]{5,4,3,2,1,0:T(8,128)(2,1)} %constant_dynamic-slice_fusion.13), channel_id=1, source_target_pairs={{0,8},{2,10},{4,12},{6,14},{8,0},{10,2},{12,4},{14,6},{16,24},{18,... | collective-permute-start | bytes 995336 | tf_op jit(solution)/shard_map/ppermute | solution.py:80
  318.0 8.2 %collective-permute-start.21 = (bf16[2,2,1,1,72,256]{5,4,3,2,1,0:T(8,128)(2,1)}, bf16[2,2,1,1,72,256]{5,4,3,2,1,0:T(8,128)(2,1)S(1)}, u32[]{:S(2)}, u32[]{:S(2)}) collective-permute-start(bf16[2,2,1,1,72,256]{5,4,3,2,1,0:T(8,128)(2,1)} %constant_dynamic-slice_fusion.22), channel_id=1, source_target_pairs={{0,4},{2,6},{4,0},{6,2},{8,12},{10,14},{12,8},{14,10},{16,20},{18,... | collective-permute-start | bytes 442376 | tf_op jit(solution)/shard_map/ppermute | solution.py:80
  331.6 10.9 %collective-permute-start.34 = (bf16[2,1,1,1,72,1152]{5,4,3,2,1,0:T(8,128)(2,1)}, bf16[2,1,1,1,72,1152]{5,4,3,2,1,0:T(8,128)(2,1)S(1)}, u32[]{:S(2)}, u32[]{:S(2)}) collective-permute-start(bf16[2,1,1,1,72,1152]{5,4,3,2,1,0:T(8,128)(2,1)} %constant_dynamic-slice_fusion.9), channel_id=1, source_target_pairs={{0,8},{2,10},{4,12},{6,14},{8,0},{10,2},{12,4},{14,6},{16,24},{18,... | collective-permute-start | bytes 995336 | tf_op jit(solution)/shard_map/ppermute | solution.py:80
  332.1 17.5 %collective-permute-start.38 = (bf16[2,1,1,1,72,1152]{5,4,3,2,1,0:T(8,128)(2,1)S(1)}, bf16[2,1,1,1,72,1152]{5,4,3,2,1,0:T(8,128)(2,1)S(1)}, u32[]{:S(2)}, u32[]{:S(2)}) collective-permute-start(bf16[2,1,1,1,72,1152]{5,4,3,2,1,0:T(8,128)(2,1)S(1)} %copy-done.40), channel_id=1, source_target_pairs={{0,8},{2,10},{4,12},{6,14},{8,0},{10,2},{12,4},{14,6},{16,24},{18,... | collective-permute-start | bytes 995336 | tf_op jit(solution)/shard_map/ppermute | solution.py:80
  342.6 11.4 %collective-permute-start.42 = (bf16[2,1,1,1,72,1152]{5,4,3,2,1,0:T(8,128)(2,1)S(1)}, bf16[2,1,1,1,72,1152]{5,4,3,2,1,0:T(8,128)(2,1)S(1)}, u32[]{:S(2)}, u32[]{:S(2)}) collective-permute-start(bf16[2,1,1,1,72,1152]{5,4,3,2,1,0:T(8,128)(2,1)S(1)} %copy-done.39), channel_id=1, source_target_pairs={{0,8},{2,10},{4,12},{6,14},{8,0},{10,2},{12,4},{14,6},{16,24},{18,... | collective-permute-start | bytes 995336 | tf_op jit(solution)/shard_map/ppermute | solution.py:80
  349.7 7.5 %collective-permute-start.25 = (bf16[2,2,1,1,72,320]{5,4,3,2,1,0:T(8,128)(2,1)S(1)}, bf16[2,2,1,1,72,320]{5,4,3,2,1,0:T(8,128)(2,1)S(1)}, u32[]{:S(2)}, u32[]{:S(2)}) collective-permute-start(bf16[2,2,1,1,72,320]{5,4,3,2,1,0:T(8,128)(2,1)S(1)} %constant_dynamic-slice_fusion.18), channel_id=1, source_target_pairs={{0,2},{2,0},{4,6},{6,4},{8,10},{10,8},{12,14},{14,12},{16,18},{18,... | collective-permute-start | bytes 552968 | tf_op jit(solution)/shard_map/ppermute | solution.py:80
  354.0 10.3 %collective-permute-start.23 = (bf16[1,1,1,1,72,256]{5,4,3,2,1,0:T(8,128)(2,1)S(1)}, bf16[1,1,1,1,72,256]{5,4,3,2,1,0:T(8,128)(2,1)S(1)}, u32[]{:S(2)}, u32[]{:S(2)}) collective-permute-start(bf16[1,1,1,1,72,256]{5,4,3,2,1,0:T(8,128)(2,1)S(1)} %constant_dynamic-slice_fusion.20), channel_id=1, source_target_pairs={{0,16},{2,18},{4,20},{6,22},{8,24},{10,26},{12,28},{14,30},{16,0},... | collective-permute-start | bytes 110600 | tf_op jit(solution)/shard_map/ppermute | solution.py:80
  357.3 5.6 %collective-permute-start.26 = (bf16[2,1,1,1,72,320]{5,4,3,2,1,0:T(8,128)(2,1)S(1)}, bf16[2,1,1,1,72,320]{5,4,3,2,1,0:T(8,128)(2,1)S(1)}, u32[]{:S(2)}, u32[]{:S(2)}) collective-permute-start(bf16[2,1,1,1,72,320]{5,4,3,2,1,0:T(8,128)(2,1)S(1)} %constant_dynamic-slice_fusion.17), channel_id=1, source_target_pairs={{0,8},{2,10},{4,12},{6,14},{8,0},{10,2},{12,4},{14,6},{16,24},{18,... | collective-permute-start | bytes 276488 | tf_op jit(solution)/shard_map/ppermute | solution.py:80
  362.9 15.7 %collective-permute-start.31 = (bf16[1,1,1,1,72,1152]{5,4,3,2,1,0:T(8,128)(2,1)S(1)}, bf16[1,1,1,1,72,1152]{5,4,3,2,1,0:T(8,128)(2,1)S(1)}, u32[]{:S(2)}, u32[]{:S(2)}) collective-permute-start(bf16[1,1,1,1,72,1152]{5,4,3,2,1,0:T(8,128)(2,1)S(1)} %constant_dynamic-slice_fusion.12), channel_id=1, source_target_pairs={{0,16},{2,18},{4,20},{6,22},{8,24},{10,26},{12,28},{14,30},{16,0},... | collective-permute-start | bytes 497672 | tf_op jit(solution)/shard_map/ppermute | solution.py:80
  364.3 13.6 %collective-permute-start.27 = (bf16[1,1,1,1,72,320]{5,4,3,2,1,0:T(8,128)(2,1)S(1)}, bf16[1,1,1,1,72,320]{5,4,3,2,1,0:T(8,128)(2,1)S(1)}, u32[]{:S(2)}, u32[]{:S(2)}) collective-permute-start(bf16[1,1,1,1,72,320]{5,4,3,2,1,0:T(8,128)(2,1)S(1)} %constant_dynamic-slice_fusion.16), channel_id=1, source_target_pairs={{0,16},{2,18},{4,20},{6,22},{8,24},{10,26},{12,28},{14,30},{16,0},... | collective-permute-start | bytes 138248 | tf_op jit(solution)/shard_map/ppermute | solution.py:80
  377.9 10.5 %collective-permute-start.35 = (bf16[1,1,1,1,72,1152]{5,4,3,2,1,0:T(8,128)(2,1)S(1)}, bf16[1,1,1,1,72,1152]{5,4,3,2,1,0:T(8,128)(2,1)S(1)}, u32[]{:S(2)}, u32[]{:S(2)}) collective-permute-start(bf16[1,1,1,1,72,1152]{5,4,3,2,1,0:T(8,128)(2,1)S(1)} %constant_dynamic-slice_fusion.8), channel_id=1, source_target_pairs={{0,16},{2,18},{4,20},{6,22},{8,24},{10,26},{12,28},{14,30},{16,0},... | collective-permute-start | bytes 497672 | tf_op jit(solution)/shard_map/ppermute | solution.py:80
  378.6 11.6 %collective-permute-start.39 = (bf16[1,1,1,1,72,1152]{5,4,3,2,1,0:T(8,128)(2,1)S(1)}, bf16[1,1,1,1,72,1152]{5,4,3,2,1,0:T(8,128)(2,1)S(1)}, u32[]{:S(2)}, u32[]{:S(2)}) collective-permute-start(bf16[1,1,1,1,72,1152]{5,4,3,2,1,0:T(8,128)(2,1)S(1)} %constant_dynamic-slice_fusion.4), channel_id=1, source_target_pairs={{0,16},{2,18},{4,20},{6,22},{8,24},{10,26},{12,28},{14,30},{16,0},... | collective-permute-start | bytes 497672 | tf_op jit(solution)/shard_map/ppermute | solution.py:80
  388.3 7.3 %collective-permute-start.43 = (bf16[1,1,1,1,72,1152]{5,4,3,2,1,0:T(8,128)(2,1)S(1)}, bf16[1,1,1,1,72,1152]{5,4,3,2,1,0:T(8,128)(2,1)S(1)}, u32[]{:S(2)}, u32[]{:S(2)}) collective-permute-start(bf16[1,1,1,1,72,1152]{5,4,3,2,1,0:T(8,128)(2,1)S(1)} %constant_dynamic-slice_fusion), channel_id=1, source_target_pairs={{0,16},{2,18},{4,20},{6,22},{8,24},{10,26},{12,28},{14,30},{16,0},... | collective-permute-start | bytes 497672 | tf_op jit(solution)/shard_map/ppermute | solution.py:80
  406.2 25.2 %collective-permute-start.6 = (bf16[1,768]{1,0:T(2,128)(2,1)S(1)}, bf16[1,768]{1,0:T(2,128)(2,1)S(1)}, u32[]{:S(2)}, u32[]{:S(2)}) collective-permute-start(bf16[1,768]{1,0:T(2,128)(2,1)S(1)} %convert_element_type.619), channel_id=1, source_target_pairs={{0,1},{1,0},{2,3},{3,2},{4,5},{5,4},{6,7},{7,6},{8,9},{9,8},{10,11... | collective-permute-start | bytes 4616 | tf_op jit(solution)/shard_map/ppermute | solution.py:40
  406.3 25.7 %collective-permute-start.5 = (bf16[1,768]{1,0:T(2,128)(2,1)S(1)}, bf16[1,768]{1,0:T(2,128)(2,1)S(1)}, u32[]{:S(2)}, u32[]{:S(2)}) collective-permute-start(bf16[1,768]{1,0:T(2,128)(2,1)S(1)} %convert_element_type.615), channel_id=1, source_target_pairs={{0,1},{1,0},{2,3},{3,2},{4,5},{5,4},{6,7},{7,6},{8,9},{9,8},{10,11... | collective-permute-start | bytes 4616 | tf_op jit(solution)/shard_map/ppermute | solution.py:40
  424.0 8.0 %collective-permute-start.7 = (bf16[1,8,1152]{2,1,0:T(8,128)(2,1)S(1)}, bf16[1,8,1152]{2,1,0:T(8,128)(2,1)S(1)}, u32[]{:S(2)}, u32[]{:S(2)}) collective-permute-start(bf16[1,8,1152]{2,1,0:T(8,128)(2,1)S(1)} %fusion.33), channel_id=1, source_target_pairs={{0,1},{1,0},{2,3},{3,2},{4,5},{5,4},{6,7},{7,6},{8,9},{9,8},{10,11... | collective-permute-start | bytes 55304 | tf_op jit(solution)/shard_map/ppermute | solution.py:40
  427.7 14.7 %collective-permute-start.48 = (bf16[1,1,8,6,576]{4,2,3,1,0:T(8,128)(2,1)S(1)}, bf16[1,1,8,6,576]{4,2,3,1,0:T(8,128)(2,1)S(1)}, u32[]{:S(2)}, u32[]{:S(2)}) collective-permute-start(bf16[1,1,8,6,576]{4,2,3,1,0:T(8,128)(2,1)S(1)} %get-tuple-element.101), channel_id=1, source_target_pairs={{0,2},{2,0},{4,6},{6,4},{8,10},{10,8},{12,14},{14,12},{16,18},{18,... | collective-permute-start | bytes 165896 | tf_op jit(solution)/shard_map/ppermute | solution.py:66
  431.4 25.7 %collective-permute-start.9 = (bf16[2,2,1,1,72,768]{5,4,3,2,1,0:T(8,128)(2,1)}, bf16[2,2,1,1,72,768]{5,4,3,2,1,0:T(8,128)(2,1)}, u32[]{:S(2)}, u32[]{:S(2)}) collective-permute-start(bf16[2,2,1,1,72,768]{5,4,3,2,1,0:T(8,128)(2,1)} %constant_dynamic-slice_fusion.30), channel_id=1, source_target_pairs={{0,4},{2,6},{4,0},{6,2},{8,12},{10,14},{12,8},{14,10},{16,20},{18,... | collective-permute-start | bytes 1327112 | tf_op jit(solution)/shard_map/ppermute | solution.py:80
  432.7 7.6 %collective-permute-start.44 = (bf16[1,1,8,1152]{3,2,1,0:T(8,128)(2,1)S(1)}, bf16[1,1,8,1152]{3,2,1,0:T(8,128)(2,1)S(1)}, u32[]{:S(2)}, u32[]{:S(2)}) collective-permute-start(bf16[1,1,8,1152]{3,2,1,0:T(8,128)(2,1)S(1)} %get-tuple-element.99), channel_id=1, source_target_pairs={{0,2},{2,0},{4,6},{6,4},{8,10},{10,8},{12,14},{14,12},{16,18},{18,... | collective-permute-start | bytes 55304 | tf_op jit(solution)/shard_map/ppermute | solution.py:66
  440.2 4.6 collective-permute-start.45
  442.4 7.6 %collective-permute-start.49 = (bf16[2,1,8,6,576]{4,2,3,1,0:T(8,128)(2,1)S(1)}, bf16[2,1,8,6,576]{4,2,3,1,0:T(8,128)(2,1)S(1)}, u32[]{:S(2)}, u32[]{:S(2)}) collective-permute-start(bf16[2,1,8,6,576]{4,2,3,1,0:T(8,128)(2,1)S(1)} %pad_maximum_fusion.6), channel_id=1, source_target_pairs={{0,4},{2,6},{4,0},{6,2},{8,12},{10,14},{12,8},{14,10},{16,20},{18,... | collective-permute-start | bytes 331784 | tf_op jit(solution)/shard_map/ppermute | solution.py:66
  449.3 7.8 %collective-permute-start.47 = (bf16[8,1,8,1152]{3,2,1,0:T(8,128)(2,1)S(1)}, bf16[8,1,8,1152]{3,2,1,0:T(8,128)(2,1)S(1)}, u32[]{:S(2)}, u32[]{:S(2)}) collective-permute-start(bf16[8,1,8,1152]{3,2,1,0:T(8,128)(2,1)S(1)} %pad_maximum_fusion.5), channel_id=1, source_target_pairs={{0,16},{2,18},{4,20},{6,22},{8,24},{10,26},{12,28},{14,30},{16,0},... | collective-permute-start | bytes 442376 | tf_op jit(solution)/shard_map/ppermute | solution.py:66
  450.1 9.7 %collective-permute-start.50 = (bf16[4,1,8,6,576]{4,2,3,1,0:T(8,128)(2,1)S(1)}, bf16[4,1,8,6,576]{4,2,3,1,0:T(8,128)(2,1)S(1)}, u32[]{:S(2)}, u32[]{:S(2)}) collective-permute-start(bf16[4,1,8,6,576]{4,2,3,1,0:T(8,128)(2,1)S(1)} %pad_maximum_fusion.3), channel_id=1, source_target_pairs={{0,8},{2,10},{4,12},{6,14},{8,0},{10,2},{12,4},{14,6},{16,24},{18,... | collective-permute-start | bytes 663560 | tf_op jit(solution)/shard_map/ppermute | solution.py:66
  455.0 13.0 %collective-permute-start.13 = (bf16[2,2,1,1,72,960]{5,4,3,2,1,0:T(8,128)(2,1)S(1)}, bf16[2,2,1,1,72,960]{5,4,3,2,1,0:T(8,128)(2,1)S(1)}, u32[]{:S(2)}, u32[]{:S(2)}) collective-permute-start(bf16[2,2,1,1,72,960]{5,4,3,2,1,0:T(8,128)(2,1)S(1)} %constant_dynamic-slice_fusion.26), channel_id=1, source_target_pairs={{0,2},{2,0},{4,6},{6,4},{8,10},{10,8},{12,14},{14,12},{16,18},{18,... | collective-permute-start | bytes 1658888 | tf_op jit(solution)/shard_map/ppermute | solution.py:80
  458.3 8.9 %collective-permute-start.10 = (bf16[2,1,1,1,72,768]{5,4,3,2,1,0:T(8,128)(2,1)S(1)}, bf16[2,1,1,1,72,768]{5,4,3,2,1,0:T(8,128)(2,1)S(1)}, u32[]{:S(2)}, u32[]{:S(2)}) collective-permute-start(bf16[2,1,1,1,72,768]{5,4,3,2,1,0:T(8,128)(2,1)S(1)} %constant_dynamic-slice_fusion.29), channel_id=1, source_target_pairs={{0,8},{2,10},{4,12},{6,14},{8,0},{10,2},{12,4},{14,6},{16,24},{18,... | collective-permute-start | bytes 663560 | tf_op jit(solution)/shard_map/ppermute | solution.py:80
  459.9 27.7 %collective-permute-start.51 = (bf16[8,1,8,6,576]{4,2,3,1,0:T(8,128)(2,1)S(1)}, bf16[8,1,8,6,576]{4,2,3,1,0:T(8,128)(2,1)S(1)}, u32[]{:S(2)}, u32[]{:S(2)}) collective-permute-start(bf16[8,1,8,6,576]{4,2,3,1,0:T(8,128)(2,1)S(1)} %pad_maximum_fusion.2), channel_id=1, source_target_pairs={{0,16},{2,18},{4,20},{6,22},{8,24},{10,26},{12,28},{14,30},{16,0},... | collective-permute-start | bytes 1327112 | tf_op jit(solution)/shard_map/ppermute | solution.py:66
  467.3 20.2 %collective-permute-start.11 = (bf16[1,1,1,1,72,768]{5,4,3,2,1,0:T(8,128)(2,1)S(1)}, bf16[1,1,1,1,72,768]{5,4,3,2,1,0:T(8,128)(2,1)S(1)}, u32[]{:S(2)}, u32[]{:S(2)}) collective-permute-start(bf16[1,1,1,1,72,768]{5,4,3,2,1,0:T(8,128)(2,1)S(1)} %constant_dynamic-slice_fusion.28), channel_id=1, source_target_pairs={{0,16},{2,18},{4,20},{6,22},{8,24},{10,26},{12,28},{14,30},{16,0},... | collective-permute-start | bytes 331784 | tf_op jit(solution)/shard_map/ppermute | solution.py:80
  468.3 20.2 %collective-permute-start.14 = (bf16[2,1,1,1,72,960]{5,4,3,2,1,0:T(8,128)(2,1)S(1)}, bf16[2,1,1,1,72,960]{5,4,3,2,1,0:T(8,128)(2,1)S(1)}, u32[]{:S(2)}, u32[]{:S(2)}) collective-permute-start(bf16[2,1,1,1,72,960]{5,4,3,2,1,0:T(8,128)(2,1)S(1)} %constant_dynamic-slice_fusion.25), channel_id=1, source_target_pairs={{0,8},{2,10},{4,12},{6,14},{8,0},{10,2},{12,4},{14,6},{16,24},{18,... | collective-permute-start | bytes 829448 | tf_op jit(solution)/shard_map/ppermute | solution.py:80
  488.6 8.0 %collective-permute-start.15 = (bf16[1,1,1,1,72,960]{5,4,3,2,1,0:T(8,128)(2,1)S(1)}, bf16[1,1,1,1,72,960]{5,4,3,2,1,0:T(8,128)(2,1)S(1)}, u32[]{:S(2)}, u32[]{:S(2)}) collective-permute-start(bf16[1,1,1,1,72,960]{5,4,3,2,1,0:T(8,128)(2,1)S(1)} %constant_dynamic-slice_fusion.24), channel_id=1, source_target_pairs={{0,16},{2,18},{4,20},{6,22},{8,24},{10,26},{12,28},{14,30},{16,0},... | collective-permute-start | bytes 414728 | tf_op jit(solution)/shard_map/ppermute | solution.py:80
  (70 other events, 641.1 us)

commit v2 on v0

v2 whole, which is shorter than its diff:
```python
import functools

import jax
import jax.numpy as jnp
from jax import lax
from jax.experimental import pallas as pl
from jax.experimental.pallas import tpu as pltpu
from jax.sharding import PartitionSpec as P

EPS = 1e-06
HIGHEST = lax.Precision.HIGHEST
HEAD_DIM = 72
SEGS = 8
MOST = 256
LOG2E = 1.4426950408889634
NEG = -1e30


def band(begin, width, length):
    low = max(0, (begin - MOST + 1) // 128 * 128)
    high = min(length, -(-(begin + width + MOST - 1) // 128) * 128)
    return low, high


def natural(array):
    return array.astype(jnp.float32).T.astype(jnp.bfloat16)


def marks(seg_row):
    slots = lax.broadcasted_iota(jnp.int32, (SEGS, seg_row.shape[-1]), 0)
    return (slots == seg_row[...]).astype(jnp.float32)


def fill(head, qkv, one_hot, q_aug, k_nat):
    query = jnp.concatenate([qkv[0, head].astype(jnp.float32), (1.0 - one_hot) * NEG], axis=0)
    q_aug[...] = query.astype(jnp.bfloat16)
    k_nat[...] = natural(jnp.concatenate([qkv[1, head].astype(jnp.float32), one_hot], axis=0))


def attention_forward_kernel(width, seg_row, qkv, out, stat, q_aug, k_nat):
    heads, length = qkv.shape[1], qkv.shape[3]
    factor = HEAD_DIM**-0.5 * LOG2E
    one_hot = marks(seg_row)

    def one(head, carry):
        fill(head, qkv, one_hot, q_aug, k_nat)
        for begin in range(0, length, width):
            low, high = band(begin, width, length)
            span = slice(begin, begin + width)
            scores = jnp.dot(
                k_nat[low:high, :], q_aug[:, span], preferred_element_type=jnp.float32
            )
            peak = jnp.max(scores, axis=0, keepdims=True) * factor
            shifted = jnp.exp2(scores * factor - peak)
            total = jnp.sum(shifted, axis=0, keepdims=True)
            got = jnp.dot(
                qkv[2, head, :, low:high],
                shifted.astype(jnp.bfloat16),
                preferred_element_type=jnp.float32,
            )
            out[head, :, span] = (got * (1.0 / total)).astype(jnp.bfloat16)
            stat[head, :, span] = peak + jnp.log2(total)
        return carry

    lax.fori_loop(0, heads, one, 0, unroll=2)


def attention_backward_kernel(
    width, seg_row, qkv, stat, grad, out, q_aug, k_nat, v_nat, q_nat, g_nat, p_all, s_all
):
    heads, length = qkv.shape[1], qkv.shape[3]
    scale = HEAD_DIM**-0.5
    factor = scale * LOG2E
    one_hot = marks(seg_row)

    def one(head, carry):
        fill(head, qkv, one_hot, q_aug, k_nat)
        v_nat[...] = natural(qkv[2, head])
        q_nat[...] = natural(qkv[0, head])
        g_nat[...] = natural(grad[head])
        for begin in range(0, length, width):
            low, high = band(begin, width, length)
            span = slice(begin, begin + width)
            scores = jnp.dot(
                k_nat[low:high, :], q_aug[:, span], preferred_element_type=jnp.float32
            )
            probs = jnp.exp2(scores * factor - stat[head, :, span])
            prob_grad = jnp.dot(
                v_nat[low:high, :], grad[head, :, span], preferred_element_type=jnp.float32
            )
            row = jnp.sum(prob_grad * probs, axis=0, keepdims=True)
            score_grad = (probs * (prob_grad - row)).astype(jnp.bfloat16)
            p_all[low:high, span] = probs.astype(jnp.bfloat16)
            s_all[low:high, span] = score_grad
            got = jnp.dot(
                qkv[1, head, :, low:high], score_grad, preferred_element_type=jnp.float32
            )
            out[0, head, :, span] = (got * scale).astype(jnp.bfloat16)
        for begin in range(0, length, width):
            span = slice(begin, begin + width)
            reach = [q for q in range(0, length, width) if band(q, width, length)[0] < begin + width and band(q, width, length)[1] > begin]
            low, high = reach[0], reach[-1] + width
            key_grad = jnp.dot(
                s_all[span, low:high], q_nat[low:high, :], preferred_element_type=jnp.float32
            )
            value_grad = jnp.dot(
                p_all[span, low:high], g_nat[low:high, :], preferred_element_type=jnp.float32
            )
            out[1, head, :, span] = (key_grad * scale).T.astype(jnp.bfloat16)
            out[2, head, :, span] = value_grad.T.astype(jnp.bfloat16)
        return carry

    if width < MOST:
        p_all[...] = jnp.zeros_like(p_all)
        s_all[...] = jnp.zeros_like(s_all)
    lax.fori_loop(0, heads, one, 0, unroll=2)


VMEM = pl.BlockSpec(memory_space=pltpu.VMEM)


def attention_forward(segments, qkv, width=256):
    heads, length = qkv.shape[1], qkv.shape[3]
    return pl.pallas_call(
        functools.partial(attention_forward_kernel, width),
        in_specs=[VMEM] * 2,
        out_specs=[VMEM] * 2,
        out_shape=[
            jax.ShapeDtypeStruct((heads, HEAD_DIM, length), jnp.bfloat16),
            jax.ShapeDtypeStruct((heads, 1, length), jnp.float32),
        ],
        scratch_shapes=[
            pltpu.VMEM((HEAD_DIM + SEGS, length), jnp.bfloat16),
            pltpu.VMEM((length, HEAD_DIM + SEGS), jnp.bfloat16),
        ],
        compiler_params=pltpu.CompilerParams(vmem_limit_bytes=32 << 20),
        cost_estimate=pl.CostEstimate(
            flops=4 * heads * length * length * HEAD_DIM,
            bytes_accessed=8 * heads * HEAD_DIM * length,
            transcendentals=heads * length * length,
        ),
    )(segments, qkv)


def attention_backward(segments, qkv, stat, grad, width=256):
    heads, length = qkv.shape[1], qkv.shape[3]
    return pl.pallas_call(
        functools.partial(attention_backward_kernel, width),
        in_specs=[VMEM] * 4,
        out_specs=VMEM,
        out_shape=jax.ShapeDtypeStruct(qkv.shape, jnp.bfloat16),
        scratch_shapes=[
            pltpu.VMEM((HEAD_DIM + SEGS, length), jnp.bfloat16),
            pltpu.VMEM((length, HEAD_DIM + SEGS), jnp.bfloat16),
            pltpu.VMEM((length, HEAD_DIM), jnp.bfloat16),
            pltpu.VMEM((length, HEAD_DIM), jnp.bfloat16),
            pltpu.VMEM((length, HEAD_DIM), jnp.bfloat16),
            pltpu.VMEM((length, length), jnp.bfloat16),
            pltpu.VMEM((length, length), jnp.bfloat16),
        ],
        compiler_params=pltpu.CompilerParams(vmem_limit_bytes=32 << 20),
        cost_estimate=pl.CostEstimate(
            flops=10 * heads * length * length * HEAD_DIM,
            bytes_accessed=14 * heads * HEAD_DIM * length,
            transcendentals=heads * length * length,
        ),
    )(segments, qkv, stat, grad)


def silu(array):
    return array / (1.0 + jnp.exp(-array))


def gelu(array):
    tanh_arg = 0.7978845608028654 * (array + 0.044715 * array * array * array)
    return 0.5 * array * (1.0 + jnp.tanh(tanh_arg))


def normalize(array):
    center = array - jnp.mean(array, axis=-1, keepdims=True)
    spread = jnp.mean(center * center, axis=-1, keepdims=True)
    inverse = lax.rsqrt(spread + EPS)
    return (center * inverse, inverse)


def product(spec, left, right):
    return jnp.einsum(spec, left, right, preferred_element_type=jnp.float32)


def segment_pick(one_hot, table):
    return jnp.einsum("ls,sc->lc", one_hot, table, precision=HIGHEST)


def segment_total(one_hot, array):
    return jnp.einsum("ls,lc->sc", one_hot, array, precision=HIGHEST)


def exchange(array):
    return lax.ppermute(array, "tensor", [(0, 1), (1, 0)])


def tensor_sum(array, size):
    if size == 2:
        return array.astype(jnp.float32) + exchange(array).astype(jnp.float32)
    return lax.psum(array, "tensor").astype(jnp.float32)


def tensor_join(array, size):
    if size == 2:
        other = exchange(array)
        first = lax.axis_index("tensor") == 0
        return jnp.concatenate(
            [jnp.where(first, array, other), jnp.where(first, other, array)], axis=-1
        )
    return lax.all_gather(array, "tensor", axis=array.ndim - 1, tiled=True)


def partners(size, bit):
    return [(i, i ^ (1 << bit)) for i in range(size)]


def tie(*values):
    return lax.optimization_barrier(values)


class Gather:
    def __init__(self, array, size, order):
        self.held, self.size, self.order = array[None], size, list(order)

    def step(self):
        if self.order:
            bit = self.order.pop(0)
            other = lax.ppermute(self.held, "batch", partners(self.size, bit))
            self.held = jnp.concatenate([self.held, other], axis=0)


class Halving:
    def __init__(self, halves, size):
        self.size, self.bits = size, size.bit_length() - 1
        self.cubes = [
            half.reshape((2,) * self.bits + (half.shape[0] // size, half.shape[1]))
            for half in halves
        ]
        self.stage = 0
        self.order = list(range(self.bits))
        self.keep = self.got = None

    def pieces(self):
        index = lax.axis_index("batch")
        keeps, sends, bits = [], [], []
        for at, cube in enumerate(self.cubes):
            bit = self.order[1 - self.stage if at == 1 and self.stage < 2 else self.stage]
            axis = self.bits - 1 - bit
            mine = (index >> bit) & 1
            sends.append(lax.dynamic_index_in_dim(cube, 1 - mine, axis, keepdims=True))
            keeps.append(lax.dynamic_index_in_dim(cube, mine, axis, keepdims=True))
            bits.append(bit)
        return keeps, sends, bits

    def send(self, *others):
        self.keep, sends, bits = self.pieces()
        tied = tie(*sends, *others)
        sends, others = tied[: len(sends)], tied[len(sends) :]
        self.got = [
            lax.ppermute(piece, "batch", partners(self.size, bit))
            for piece, bit in zip(sends, bits)
        ]
        return others

    def take(self, *others):
        tied = tie(*self.got, *others)
        got, others = tied[: len(self.got)], tied[len(self.got) :]
        self.stage += 1
        last = self.stage == self.bits
        self.cubes = []
        for keep, new in zip(self.keep, got):
            total = keep.astype(jnp.float32) + new.astype(jnp.float32)
            self.cubes.append(total if last else total.astype(jnp.bfloat16))
        if self.stage == 2:
            self.cubes = [jnp.concatenate(self.cubes, axis=-1)]
        return others

    def result(self):
        while self.stage < self.bits:
            self.send()
            self.take()
        return self.cubes[0].reshape(self.cubes[0].shape[-2:])


def high_low(array):
    high = array.astype(jnp.bfloat16)
    return [high, (array - high.astype(jnp.float32)).astype(jnp.bfloat16)]


def on_device(
    n_batch,
    tokens,
    segment_ids,
    conditions,
    condition_segment,
    qkv_weight,
    qv_bias,
    proj_weight,
    proj_bias,
    up_weight,
    up_bias,
    down_weight,
    down_bias,
    mod_weight,
    mod_bias,
    out_grad,
):
    bf16, f32 = jnp.bfloat16, jnp.float32
    length, model_width = tokens.shape[1:]
    local_width = qkv_weight.shape[2]
    hidden_width = up_weight.shape[1]
    heads = local_width // HEAD_DIM
    n_tensor = model_width // local_width
    offset = lax.axis_index("tensor") * local_width
    bits = list(range(n_batch.bit_length() - 1))

    def mine(array):
        return lax.dynamic_slice_in_dim(array, offset, local_width, 1)

    cond_float = conditions[0].astype(f32)
    cond_act = silu(cond_float).astype(bf16)
    mod_local = product("sd,djc->sjc", cond_act, mod_weight) + mod_bias
    modulation = tensor_join(mod_local, n_tensor)
    one_hot = (segment_ids[0][:, None] == condition_segment[0][None, :]).astype(f32)
    shift_one = segment_pick(one_hot, modulation[:, 0])
    scale_one = segment_pick(one_hot, modulation[:, 1])
    gate_one = segment_pick(one_hot, modulation[:, 2])
    shift_two = segment_pick(one_hot, modulation[:, 3])
    scale_two = segment_pick(one_hot, modulation[:, 4])
    gate_two = segment_pick(one_hot, modulation[:, 5])
    tok_float = tokens[0].astype(f32)
    normed_one, inverse_one = normalize(tok_float)
    attn_in = (normed_one * (1.0 + scale_one) + shift_one).astype(bf16)
    biases = jnp.stack([qv_bias[0], jnp.zeros_like(qv_bias[0]), qv_bias[1]])
    qkv = product("djc,ld->jcl", qkv_weight, attn_in) + biases[:, :, None]
    qkv = qkv.astype(bf16).reshape((3, heads, HEAD_DIM, length))
    attended, stat = attention_forward(segment_ids, qkv)
    attended = attended.reshape((local_width, length))
    proj_part = product("cl,cd->ld", attended, proj_weight).astype(bf16)
    attn_out = tensor_sum(proj_part, n_tensor) + proj_bias
    middle = tok_float + gate_one * attn_out
    normed_two, inverse_two = normalize(middle)
    mlp_in = (normed_two * (1.0 + scale_two) + shift_two).astype(bf16)
    hidden = product("ld,df->lf", mlp_in, up_weight) + up_bias
    active = gelu(hidden).astype(bf16)
    grad_float = out_grad[0].astype(f32)
    mlp_grad = (grad_float * gate_two).astype(bf16)
    down_bias_grad = jnp.sum(mlp_grad.astype(f32), axis=0)

    cut = hidden_width // 2

    def weight_grad(left, right):
        return product("ld,lc->dc", left, right).astype(bf16)

    down_sum = Halving([weight_grad(mlp_grad, active[:, :cut]), weight_grad(mlp_grad, active[:, cut:])], n_batch)
    (mlp_grad_then,) = down_sum.send(mlp_grad)
    active_grad = product("ld,fd->lf", mlp_grad_then, down_weight)
    hidden_grad = jax.vjp(gelu, hidden)[1](active_grad)[0].astype(bf16)
    up_bias_grad = jnp.sum(hidden_grad.astype(f32), axis=0)
    mlp_part = product("lf,df->ld", hidden_grad, up_weight).astype(bf16)
    up_halves = [weight_grad(mlp_in, hidden_grad[:, :cut]), weight_grad(mlp_in, hidden_grad[:, cut:])]
    mlp_in_grad = tensor_sum(mlp_part, n_tensor)
    up_first, up_second = down_sum.take(*up_halves)
    (mlp_in_grad,) = down_sum.send(mlp_in_grad)
    scale_two_grad = mlp_in_grad * normed_two
    scaled_two = mlp_in_grad * (1.0 + scale_two)
    middle_grad = grad_float + inverse_two * (
        scaled_two
        - jnp.mean(scaled_two, axis=-1, keepdims=True)
        - normed_two * jnp.mean(scaled_two * normed_two, axis=-1, keepdims=True)
    )
    attn_grad = (middle_grad * gate_one).astype(bf16)
    proj_bias_grad = jnp.sum(attn_grad.astype(f32), axis=0)
    attended_grad = product("ld,cd->cl", attn_grad, proj_weight).astype(bf16)
    proj_half = product("ld,cl->dc", attn_grad, attended).astype(bf16)

    (attended_grad,) = down_sum.take(attended_grad)
    up_sum = Halving([up_first, up_second], n_batch)
    (attended_grad,) = up_sum.send(attended_grad)
    (attended_grad,) = down_sum.send(attended_grad)
    triple = attention_backward(
        segment_ids, qkv, stat, attended_grad.reshape((heads, HEAD_DIM, length))
    ).reshape((3, local_width, length))
    (triple,) = up_sum.take(triple)
    (triple,) = down_sum.take(triple)
    (triple,) = up_sum.send(triple)
    (triple,) = down_sum.send(triple)
    qv_bias_grad = jnp.sum(triple[0::2].astype(f32), axis=2)
    both = triple[:2].reshape((2 * local_width, length))
    first_half = product("ld,cl->dc", attn_in, both).astype(bf16)
    value_half = product("ld,cl->dc", attn_in, triple[2]).astype(bf16)
    second_half = jnp.concatenate([value_half, proj_half], axis=1)
    first_half, second_half = up_sum.take(first_half, second_half)
    first_half, second_half = down_sum.take(first_half, second_half)
    qkv_sum = Halving([first_half, second_half], n_batch)
    (triple,) = qkv_sum.send(triple)
    (triple,) = up_sum.send(triple)
    attn_part = product("jcl,djc->ld", triple, qkv_weight).astype(bf16)
    if n_tensor == 2:
        sent = lax.dynamic_slice_in_dim(attn_part, local_width - offset, local_width, 1)
        attn_in_grad = mine(attn_part).astype(f32) + exchange(sent).astype(f32)
    else:
        attn_in_grad = lax.psum_scatter(
            attn_part, "tensor", scatter_dimension=1, tiled=True
        ).astype(f32)
    normed_mine = mine(normed_one)
    scaled_one = attn_in_grad * (1.0 + mine(scale_one))
    row_sums = jnp.sum(scaled_one, axis=-1)
    cross_sums = jnp.sum(scaled_one * normed_mine, axis=-1)

    (active_then, row_sums) = tie(active, row_sums)
    down_part = product("lf,fd->ld", active_then, down_weight).astype(bf16)
    mlp_out = tensor_sum(down_part, n_tensor) + down_bias
    layer_out = (middle + gate_two * mlp_out).astype(bf16)
    gate_two_grad = grad_float * mlp_out
    early_parts = (
        mine(middle_grad * attn_out),
        mine(mlp_in_grad),
        mine(scale_two_grad),
        mine(gate_two_grad),
    )
    early_tgrad = jnp.stack([segment_total(one_hot, part) for part in early_parts]).astype(bf16)
    late_parts = (attn_in_grad, attn_in_grad * normed_mine)
    late_tgrad = jnp.stack([segment_total(one_hot, part) for part in late_parts]).astype(bf16)
    row_whole = tensor_sum(row_sums.astype(bf16), n_tensor)
    cross_whole = tensor_sum(cross_sums.astype(bf16), n_tensor)
    token_grad = mine(middle_grad) + inverse_one * (
        scaled_one
        - row_whole[:, None] / model_width
        - normed_mine * (cross_whole[:, None] / model_width)
    )
    cond_part = product("jsc,djc->sd", jnp.concatenate([late_tgrad, early_tgrad]), mod_weight)
    cond_act_grad = tensor_sum(cond_part.astype(bf16), n_tensor)
    condition_grad = jax.vjp(silu, cond_float)[1](cond_act_grad)[0]

    early_bias = jnp.concatenate([proj_bias_grad, down_bias_grad, up_bias_grad])
    early = [early_tgrad, cond_act] + high_low(early_bias)
    late = [late_tgrad] + high_low(qv_bias_grad)

    def packed(arrays):
        return jnp.concatenate([array.reshape((-1, local_width)) for array in arrays], axis=0)

    order = bits[:1:-1] + bits[1::-1]
    early_all = Gather(packed(early), n_batch, order)
    late_all = Gather(packed(late), n_batch, order)

    (early_all.held,) = qkv_sum.take(early_all.held)
    (early_all.held,) = up_sum.take(early_all.held)
    (early_all.held,) = qkv_sum.send(early_all.held)
    (early_all.held,) = up_sum.send(early_all.held)
    early_all.step()
    early_all.step()
    late_all.step()
    late_all.step()
    (early_all.held, late_all.held) = qkv_sum.take(early_all.held, late_all.held)
    (early_all.held, late_all.held) = up_sum.take(early_all.held, late_all.held)
    (early_all.held, late_all.held) = qkv_sum.send(early_all.held, late_all.held)
    while early_all.order:
        early_all.step()
        late_all.step()
    (early_all.held, late_all.held) = qkv_sum.take(early_all.held, late_all.held)
    qkv_sum.send()
    segs = one_hot.shape[1]
    block = model_width // n_batch
    early_all, late_all = early_all.held, late_all.held
    early_tall = early_all[:, : 4 * segs].reshape((n_batch, 4, segs, local_width))
    cond_all = early_all[:, 4 * segs : (4 + n_tensor) * segs].reshape((n_batch, segs, model_width))
    bias_all = early_all[:, (4 + n_tensor) * segs :]
    late_tall = late_all[:, : 2 * segs].reshape((n_batch, 2, segs, local_width))
    late_bias = late_all[:, 2 * segs :]

    def bias_sum(held):
        return jnp.sum(held.astype(f32), axis=0).reshape((2, -1)).sum(axis=0)

    bias_all = bias_sum(bias_all)
    qv_sum = bias_sum(late_bias).reshape((2, local_width))
    projbias_sum = bias_all[:model_width]
    downbias_sum = bias_all[model_width : 2 * model_width]
    upbias_sum = bias_all[2 * model_width :]
    tgrad_all = jnp.concatenate([late_tall, early_tall], axis=1)
    cond_block = lax.dynamic_slice_in_dim(cond_all, lax.axis_index("batch") * block, block, 2)
    mod_sum = product("psd,pjsc->djc", cond_block, tgrad_all)
    modbias_sum = jnp.sum(tgrad_all.astype(f32), axis=(0, 2))

    qkv_sum.take()
    last = qkv_sum.result()
    down = down_sum.result().T
    up = up_sum.result()
    return (
        layer_out[None],
        token_grad[None],
        condition_grad[None],
        last[:, : 3 * local_width].reshape((-1, 3, local_width)),
        qv_sum,
        last[:, 3 * local_width :].T,
        projbias_sum,
        up,
        upbias_sum,
        down,
        downbias_sum,
        mod_sum,
        modbias_sum,
    )


def solution(mesh):
    return jax.shard_map(
        functools.partial(on_device, mesh.shape["batch"]),
        mesh=mesh,
        in_specs=(
            P("batch", None, None),
            P("batch", None),
            P("batch", None, None),
            P("batch", None),
            P(None, None, "tensor"),
            P(None, "tensor"),
            P("tensor", None),
            P(),
            P(None, "tensor"),
            P("tensor"),
            P("tensor", None),
            P(),
            P(None, None, "tensor"),
            P(None, "tensor"),
            P("batch", None, None),
        ),
        out_specs=(
            P("batch", None, None),
            P("batch", None, "tensor"),
            P("batch", None, None),
            P("batch", None, "tensor"),
            P(None, "tensor"),
            P("tensor", "batch"),
            P(),
            P("batch", "tensor"),
            P("tensor"),
            P("tensor", "batch"),
            P(),
            P("batch", None, "tensor"),
            P(None, "tensor"),
        ),
        check_vma=False,
    )
```

time: 1120 us -> 354 us (0.32)
  waiting for transfers between devices: 672 us -> 61.1 us
  blocking collectives: 104 us -> 0 us
  matrix products: 175 us -> 117 us
  starting transfers between devices: 0.5 us -> 47.3 us
  local copies, waits for them, and re-layouts: 76.6 us -> 39.5 us
  Pallas kernels: 0 us -> 27.8 us
  other arithmetic: 68.8 us -> 54.9 us
  between operations: 15.7 us -> 2.24 us
    unnamed x12 -> x0, waiting for transfers between devices: 441 us -> none
    reduce_scatter x2 -> x0, waiting for transfers between devices: 190 us -> none  [the longest x1 143 us: on_device(): lax.psum_scatter(up_weight_grad.astype(jnp.bfloat16), 'batch', scatter_di...]
    psum x2 -> x0, blocking collectives: 80.3 us -> none  [the longest x1 76.6 us: on_device(): lax.psum((qv_bias_grad, proj_bias_grad, up_bias_grad, down_bias_grad, mod...]
    ppermute x0 -> x34, waiting for transfers between devices: none -> 61.1 us  [the longest x18 33.4 us: send(): lax.ppermute(piece, 'batch', partners(self.size, bit))]
    dot_general x33 -> x30, matrix products: 175 us -> 117 us  [the longest x18 79.5 us: product(): return jnp.einsum(spec, left, right, preferred_element_type=jnp.float32)]
    unnamed x116 -> x170, local copies, waits for them, and re-layouts: 67.5 us -> 14.6 us
    ppermute x0 -> x34, starting transfers between devices: none -> 47.3 us  [the longest x8 24.7 us: step(): other = lax.ppermute(self.held, 'batch', partners(self.size, bit))]
    psum x2 -> x0, waiting for transfers between devices: 40.3 us -> none  [the longest x1 25.3 us: on_device(): lax.psum(down_part.astype(jnp.bfloat16), 'tensor').astype(jnp.float32)]
  transfers between devices with their start and end apart: 8 -> 34, of which waited for: 7 -> 16; matrix products, arithmetic and copies ran while one was open for 12% -> 33% of each run, Pallas kernels for 0% -> 5%
where the time goes in v2:
time: 354 us; the launch traced here: 350 us
  matrix products  117 us (33%)
  waiting for transfers between devices  61.1 us (17%)
  other arithmetic  54.9 us (16%)
  starting transfers between devices  47.3 us (13%)
  local copies, waits for them, and re-layouts  39.5 us (11%)
  Pallas kernels  27.8 us (8%)
    dot_general x18, matrix products, product(): return jnp.einsum(spec, left, right, preferred_element_type=jnp.float32)  79.5 us
    ppermute x18, waiting for transfers between devices, send(): lax.ppermute(piece, 'batch', partners(self.size, bit))  33.4 us
    ppermute x8, waiting for transfers between devices, step(): other = lax.ppermute(self.held, 'batch', partners(self.size, bit))  26.5 us
    ppermute x8, starting transfers between devices, step(): other = lax.ppermute(self.held, 'batch', partners(self.size, bit))  24.7 us
    dot_general x6, matrix products, segment_pick(): return jnp.einsum('ls,sc->lc', one_hot, table, precision=HIGHEST)  22.3 us
    ppermute x18, starting transfers between devices, send(): lax.ppermute(piece, 'batch', partners(self.size, bit))  21.2 us
    convert_element_type x15, other arithmetic, take(): self.cubes.append(total if last else total.astype(jnp.bfloat16))  16.5 us
    pallas_call x1, Pallas kernels, attention_backward(): pl.pallas_call(functools.partial(attention_backward_kernel, width), in_sp...  16.1 us
  transfers between devices with their start and end apart: 34, of which 16 were waited for; matrix products, arithmetic and copies ran while one was open for 33% of the time, Pallas kernels for 5%

profile of v2, /device:TPU:0, one launch (start us, length us, event | category | flops | bytes accessed | tf_op | source)
XLA Modules:
  0.0 350.2 jit_solution(5482186484320761976)
XLA Ops:
  0.7 5.7 %convolution_add_fusion.3 = f32[8,6,576]{2,0,1:T(8,128)S(1)} fusion(bf16[1152,6,576]{0,2,1:T(8,128)(2,1)} %param.27, f32[6,576]{1,0:T(8,128)} %param.28, bf16[1,8,1152]{2,1,0:T(8,128)(2,1)} %param.17), kind=kOutput, calls=%fused_computation.127 | convolution fusion | flops 63774720 | bytes 8105472 | tf_op jit(solution)/shard_map/sd,djc->sjc/dot_general | solution.py:187
  8.1 3.4 fusion.46
  11.5 4.5 %fusion.15 = bf16[768,1152]{1,0:T(8,128)(2,1)S(1)} fusion(f32[768,1152]{1,0:T(8,128)} %fusion.46, s32[8]{0:T(128)S(1)} %bitcast.202, s32[768]{0:T(1024)S(1)} %reduce.1, f32[8,6,576]{2,0,1:T(8,128)S(1)} %get-tuple-element.222, f32[8,6,576]{2,0,1:T(8,128)S(1)} %get-tuple-element.221, f32[768]{0:T(1024)S(1)} %add_rsqrt_fusion.1, ...), kind=kOutput, calls=%fused_computation.44 | convolution fusion | flops 91143168 | bytes 7308320 | tf_op jit(solution)/shard_map/ls,sc->lc/dot_general | solution.py:191
  16.1 3.9 %add_convert_fusion = bf16[768,3,576]{0,2,1:T(8,128)(2,1)S(1)} fusion(f32[3,576]{1,0:T(4,128)S(1)} %pad_maximum_fusion.13, bf16[1152,3,576]{0,2,1:T(8,128)(2,1)S(1)} %copy-done.73, bf16[768,1152]{1,0:T(8,128)(2,1)S(1)} %fusion.15), kind=kOutput, calls=%fused_computation.18 | convolution fusion | flops 3060301824 | bytes 8411904 | tf_op jit(solution)/shard_map/djc,ld->jcl/dot_general | solution.py:187
  20.0 11.7 %shard_map.246 = (bf16[8,72,768]{2,1,0:T(8,128)(2,1)S(1)}, f32[8,1,768]{2,1,0:T(1,128)S(1)}) custom-call(s32[1,768]{1,0:T(1,128)S(1)} %copy-done.2, bf16[3,8,72,768]{3,2,1,0:T(8,128)(2,1)S(1)} %bitcast.177), custom_call_target="tpu_custom_call" | custom-call | flops 1358954496 | bytes 3538944 | tf_op jit(solution)/shard_map/pallas_call | solution.py:124
  31.8 2.9 convolution_convert_fusion.5
  35.6 3.5 %bitcast_convert_fusion = f32[768,1152]{1,0:T(8,128)} fusion(bf16[1,768,1152]{2,1,0:T(8,128)(2,1)} %param.29), kind=kLoop, calls=%fused_computation.83 | loop fusion | flops 884736 | bytes 5308416 | tf_op jit(solution)/shard_map/convert_element_type | solution.py:351
  40.7 3.6 %convert_reduce_fusion.3 = (f32[1152]{0:T(1024)S(1)}, bf16[768,1152]{1,0:T(8,128)(2,1)S(1)}, f32[768,1152]{1,0:T(8,128)}) fusion(bf16[1,768,1152]{2,1,0:T(8,128)(2,1)S(1)} %copy-done.13, f32[8,6,576]{2,0,1:T(8,128)S(1)} %get-tuple-element.222, f32[8,6,576]{2,0,1:T(8,128)S(1)} %get-tuple-element.221, s32[8]{0:T(128)S(1)} %bitcast.204, s32[768]{0:T(1024)S(1)} %reduce.1), kind=kOutput, calls=%fused_computation.31 | convolution fusion | flops 89372544 | bytes 7306784 | tf_op jit(solution)/shard_map/ls,sc->lc/dot_general | solution.py:191
  44.3 7.5 %fusion.156 = (f32[768]{0:T(1024)S(1)}, f32[768,1152]{1,0:T(8,128)S(1)}, f32[768,1152]{1,0:T(8,128)}, f32[768,1152]{1,0:T(8,128)}, f32[768,1152]{1,0:T(8,128)S(1)}) fusion(bf16[1,768,1152]{2,1,0:T(8,128)(2,1)S(1)} %copy-done.11, f32[1152]{0:T(1024)S(1)} %copy-done.71, bf16[768,1152]{1,0:T(8,128)(2,1)} %collective-permute-done.1, ...), kind=kOutput, calls=%fused_computation.274 | convolution fusion | flops 93796608 | bytes 19702304 | tf_op jit(solution)/shard_map/ls,sc->lc/dot_general | solution.py:191
  55.5 7.7 %fusion.7 = (bf16[768,2304]{1,0:T(8,128)(2,1)S(1)}, f32[768,2304]{1,0:T(8,128)}) fusion(f32[2304]{0:T(1024)S(1)} %copy-done.75, bf16[768,1152]{1,0:T(8,128)(2,1)S(1)} %fusion.13, bf16[1152,2304]{1,0:T(8,128)(2,1)S(1)} %bitcast.214), kind=kOutput, calls=%fused_computation.17 | convolution fusion | flops 4094558208 | bytes 17703936 | tf_op jit(solution)/shard_map/ld,df->lf/dot_general | solution.py:187
  65.0 2.5 convolution_convert_fusion.3
  67.6 5.0 %convolution_convert_fusion.4 = bf16[1152,1152]{1,0:T(8,128)(2,1)S(1)} fusion(bf16[768,1152]{1,0:T(8,128)(2,1)S(1)} %get-tuple-element.83, bf16[768,2304]{1,0:T(8,128)(2,1)} %copy-done.76), kind=kOutput, calls=%fused_computation.8 | convolution fusion | flops 2039758848 | bytes 6193152 | tf_op jit(solution)/shard_map/ld,lc->dc/dot_general | solution.py:187
  74.5 2.8 collective-permute-start.2
  78.8 12.1 %convert_reduce_fusion = (f32[2304]{0:T(1024)S(1)}, bf16[768,2304]{1,0:T(8,128)(2,1)S(1)}) fusion(f32[768,2304]{1,0:T(8,128)} %get-tuple-element.229, f32[2304]{0:T(1024)S(1)} %copy-done.75, bf16[768,1152]{1,0:T(8,128)(2,1)S(1)} %copy-done.49, bf16[2304,1152]{1,0:T(8,128)(2,1)} %param.25), kind=kOutput, calls=%fused_computation.15 | convolution fusion | flops 4124636928 | bytes 17713152 | tf_op jit(solution)/shard_map/ld,fd->lf/dot_general | solution.py:187
  91.0 8.6 %convolution_convert_fusion.7 = bf16[768,1152]{1,0:T(8,128)(2,1)S(1)} fusion(bf16[768,2304]{1,0:T(8,128)(2,1)S(1)} %get-tuple-element.213, bf16[1152,2304]{1,0:T(8,128)(2,1)} %param.23), kind=kOutput, calls=%fused_computation.47 | convolution fusion | flops 4077748224 | bytes 10616832 | tf_op jit(solution)/shard_map/lf,df->ld/dot_general | solution.py:187
  99.7 4.1 %convolution_convert_fusion.1 = bf16[1152,1152]{1,0:T(8,128)(2,1)S(1)} fusion(bf16[768,1152]{1,0:T(8,128)(2,1)S(1)} %copy-done.51, bf16[768,2304]{1,0:T(8,128)(2,1)} %copy-done.78), kind=kOutput, calls=%fused_computation.5 | convolution fusion | flops 2039758848 | bytes 6193152 | tf_op jit(solution)/shard_map/ld,lc->dc/dot_general | solution.py:187
  103.8 2.5 convolution_convert_fusion.2
  120.1 2.8 convert_reduce_fusion.4
  123.0 2.5 fusion.67
  126.8 7.8 %collective-permute-done.5 = bf16[2,2,1,1,72,1152]{5,4,3,2,1,0:T(8,128)(2,1)S(1)} collective-permute-done((bf16[2,2,1,1,72,1152]{5,4,3,2,1,0:T(8,128)(2,1)}, bf16[2,2,1,1,72,1152]{5,4,3,2,1,0:T(8,128)(2,1)S(1)}, u32[]{:S(2)}, u32[]{:S(2)}) %collective-permute-start.5) | collective-permute-done | bytes 663584 | tf_op jit(solution)/shard_map/ppermute | solution.py:265
  140.3 2.9 convolution_convert_fusion.8
  143.3 16.1 %shard_map.247 = bf16[3,8,72,768]{3,2,1,0:T(8,128)(2,1)S(1)} custom-call(s32[1,768]{1,0:T(1,128)S(1)} %copy-done.2, bf16[3,8,72,768]{3,2,1,0:T(8,128)(2,1)S(1)} %bitcast.178, f32[8,1,768]{2,1,0:T(1,128)S(1)} %copy-done.6, bf16[8,72,768]{2,1,0:T(8,128)(2,1)S(1)} %bitcast.181), custom_call_target="tpu_custom_call" | custom-call | flops 3397386240 | bytes 6193152 | tf_op jit(solution)/shard_map/pallas_call | solution.py:147
  159.4 5.5 %collective-permute-done.7 = bf16[2,2,2,1,72,1152]{5,4,3,2,1,0:T(8,128)(2,1)} collective-permute-done((bf16[2,2,2,1,72,1152]{5,4,3,2,1,0:T(8,128)(2,1)}, bf16[2,2,2,1,72,1152]{5,4,3,2,1,0:T(8,128)(2,1)}, u32[]{:S(2)}, u32[]{:S(2)}) %collective-permute-start.7) | collective-permute-done | bytes 1327136 | tf_op jit(solution)/shard_map/ppermute | solution.py:265
  176.2 2.6 collective-permute-start.12
  180.5 4.0 %convolution_convert_fusion = bf16[1152,1152]{1,0:T(8,128)(2,1)} fusion(bf16[768,1152]{1,0:T(8,128)(2,1)S(1)} %copy-done.47, bf16[1152,768]{1,0:T(8,128)(2,1)S(1)} %bitcast.200), kind=kOutput, calls=%fused_computation.4 | convolution fusion | flops 2039758848 | bytes 6193152 | tf_op jit(solution)/shard_map/ld,cl->dc/dot_general | solution.py:187
  184.6 3.0 collective-permute-done.10
  190.6 5.2 %copy.47 = bf16[1152,1152]{1,0:T(8,128)(2,1)} copy(bf16[1152,1152]{0,1:T(8,128)(2,1)} %pad_maximum_fusion) | data formatting | bytes 5308416 | tf_op jit(solution)/shard_map/optimization_barrier | solution.py:223
  195.8 2.6 constant_dynamic-slice_fusion.6
  203.0 3.8 %fusion.14 = bf16[768,1152]{1,0:T(8,128)(2,1)S(1)} fusion(bf16[3,576,768]{2,1,0:T(8,128)(2,1)S(1)} %bitcast.175, bf16[1152,3,576]{0,2,1:T(8,128)(2,1)S(1)} %copy-done.74), kind=kOutput, calls=%fused_computation.43 | convolution fusion | flops 3058532352 | bytes 8404992 | tf_op jit(solution)/shard_map/jcl,djc->ld/dot_general | solution.py:187
  209.5 2.3 copy.48
  211.9 3.6 %fusion.54 = bf16[1,8,576]{2,1,0:T(8,128)(2,1)} fusion(f32[768,1152]{1,0:T(8,128)} %copy-done.9, s32[]{:T(128)S(6)} %select_n.96, s32[8]{0:T(128)S(1)} %bitcast.208, s32[768]{0:T(1024)S(1)} %reduce.1), kind=kOutput, calls=%fused_computation.129 | convolution fusion | flops 42473472 | bytes 1978404 | tf_op jit(solution)/shard_map/ls,lc->sc/dot_general | solution.py:195
  215.4 4.8 %fusion.64 = bf16[1,8,576]{2,1,0:T(8,128)(2,1)} fusion(f32[768,1152]{1,0:T(8,128)} %get-tuple-element.219, s32[]{:T(128)S(6)} %select_n.96, f32[768,1152]{1,0:T(8,128)} %get-tuple-element.209, s32[8]{0:T(128)S(1)} %bitcast.209, s32[768]{0:T(1024)S(1)} %reduce.1), kind=kOutput, calls=%fused_computation.131 | convolution fusion | flops 42915840 | bytes 3944484 | tf_op jit(solution)/shard_map/ls,lc->sc/dot_general | solution.py:195
  225.6 4.6 %multiply_reduce_fusion.2 = (bf16[768]{0:T(1024)(128)(2,1)S(1)}, bf16[768]{0:T(1024)(128)(2,1)S(1)}) fusion(f32[768,1152]{1,0:T(8,128)} %get-tuple-element.220, s32[]{:T(128)S(6)} %select_n.96, f32[768,1152]{1,0:T(8,128)} %fusion.46, bf16[768,576]{1,0:T(8,128)(2,1)S(1)} %copy.49, bf16[768,1152]{1,0:T(8,128)(2,1)} %copy-done.15), kind=kLoop, calls=%fused_computation.71 | loop fusion | flops 3537408 | bytes 5311492 | tf_op jit(solution)/shard_map/reduce_sum | solution.py:414
  230.3 8.6 %convolution_convert_fusion.6 = bf16[768,1152]{1,0:T(8,128)(2,1)} fusion(bf16[768,2304]{1,0:T(8,128)(2,1)S(1)} %copy-done.77, bf16[2304,1152]{1,0:T(8,128)(2,1)} %param.25), kind=kOutput, calls=%fused_computation.46 | convolution fusion | flops 4077748224 | bytes 10616832 | tf_op jit(solution)/shard_map/lf,fd->ld/dot_general | solution.py:187
  245.9 2.6 collective-permute-start.25
  248.5 2.5 collective-permute-done.25
  252.0 5.5 %add_bitcast_fusion = f32[1,768,576]{2,1,0:T(8,128)} fusion(f32[768,1152]{1,0:T(8,128)S(1)} %copy-done.14, s32[]{:T(128)S(6)} %select_n.96, f32[768,1152]{1,0:T(8,128)S(1)} %copy-done.12, f32[768]{0:T(1024)S(1)} %add_multiply_fusion.2, f32[768]{0:T(1024)S(1)} %add_multiply_fusion.3, f32[768]{0:T(1024)S(1)} %add_rsqrt_fusion.1, f32[768,1152]{1,0:T(8,128)} %fusion.46, ...), kind=kLoop, calls=%fused_computation.70 | loop fusion | flops 4423680 | bytes 8856580 | tf_op jit(solution)/shard_map/broadcast_in_dim | solution.py:496
  257.5 3.1 copy.53
  261.6 5.2 %fusion.27 = (bf16[1,768,1152]{2,1,0:T(8,128)(2,1)}, f32[768,1152]{1,0:T(8,128)S(1)}) fusion(f32[768,1152]{1,0:T(8,128)S(1)} %copy-done.8, f32[768,1152]{1,0:T(8,128)} %get-tuple-element.230, f32[1152]{0:T(1024)} %param.26, bf16[768,1152]{1,0:T(8,128)(2,1)} %collective-permute-done.14, bf16[768,1152]{1,0:T(8,128)(2,1)} %convolution_convert_fusion.6), kind=kLoop, calls=%fused_computation.78 | loop fusion | flops 6193152 | bytes 15929856 | tf_op jit(solution)/shard_map/broadcast_in_dim | solution.py:495
  274.3 2.5 collective-permute-start.23
  280.0 7.9 %collective-permute-start.24 = (bf16[2,64,576]{2,1,0:T(8,128)(2,1)S(1)}, bf16[2,64,576]{2,1,0:T(8,128)(2,1)S(1)}, u32[]{:S(2)}, u32[]{:S(2)}) collective-permute-start(bf16[2,64,576]{2,1,0:T(8,128)(2,1)S(1)} %pad_maximum_fusion.8), channel_id=1, source_target_pairs={{0,8},{2,10},{4,12},{6,14},{8,0},{10,2},{12,4},{14,6},{16,24},{18,... | collective-permute-start | bytes 442376 | tf_op jit(solution)/shard_map/ppermute | solution.py:233
  289.1 6.4 %collective-permute-done.24 = bf16[2,64,576]{2,1,0:T(8,128)(2,1)S(1)} collective-permute-done((bf16[2,64,576]{2,1,0:T(8,128)(2,1)S(1)}, bf16[2,64,576]{2,1,0:T(8,128)(2,1)S(1)}, u32[]{:S(2)}, u32[]{:S(2)}) %collective-permute-start.24) | collective-permute-done | bytes 147488 | tf_op jit(solution)/shard_map/ppermute | solution.py:233
  296.1 2.2 collective-permute-start.31
  299.1 3.5 %collective-permute-done.31 = bf16[4,20,576]{2,1,0:T(8,128)(2,1)S(1)} collective-permute-done((bf16[4,20,576]{2,1,0:T(8,128)(2,1)S(1)}, bf16[4,20,576]{2,1,0:T(8,128)(2,1)S(1)}, u32[]{:S(2)}, u32[]{:S(2)}) %collective-permute-start.31) | collective-permute-done | bytes 92192 | tf_op jit(solution)/shard_map/ppermute | solution.py:233
  302.6 3.4 collective-permute-start.32
  306.7 5.7 %collective-permute-start.30 = (bf16[8,64,576]{2,1,0:T(8,128)(2,1)S(1)}, bf16[8,64,576]{2,1,0:T(8,128)(2,1)S(1)}, u32[]{:S(2)}, u32[]{:S(2)}) collective-permute-start(bf16[8,64,576]{2,1,0:T(8,128)(2,1)S(1)} %pad_maximum_fusion.3), channel_id=1, source_target_pairs={{0,2},{2,0},{4,6},{6,4},{8,10},{10,8},{12,14},{14,12},{16,18},{18,... | collective-permute-start | bytes 1769480 | tf_op jit(solution)/shard_map/ppermute | solution.py:233
  313.4 13.4 %collective-permute-done.30 = bf16[8,64,576]{2,1,0:T(8,128)(2,1)S(1)} collective-permute-done((bf16[8,64,576]{2,1,0:T(8,128)(2,1)S(1)}, bf16[8,64,576]{2,1,0:T(8,128)(2,1)S(1)}, u32[]{:S(2)}, u32[]{:S(2)}) %collective-permute-start.30) | collective-permute-done | bytes 589856 | tf_op jit(solution)/shard_map/ppermute | solution.py:233
  335.1 11.8 %collective-permute-done.33 = bf16[1,1,1,1,72,2304]{5,4,3,2,1,0:T(8,128)(2,1)} collective-permute-done((bf16[1,1,1,1,72,2304]{5,4,3,2,1,0:T(8,128)(2,1)}, bf16[1,1,1,1,72,2304]{5,4,3,2,1,0:T(8,128)(2,1)}, u32[]{:S(2)}, u32[]{:S(2)}) %collective-permute-start.33) | collective-permute-done | bytes 331808 | tf_op jit(solution)/shard_map/ppermute | solution.py:265
  (331 shorter events, 97.6 us)
Async XLA Ops:
  0.6 31.1 %copy-start = (bf16[576,1152]{1,0:T(8,128)(2,1)S(1)}, bf16[576,1152]{1,0:T(8,128)(2,1)}, u32[]{:S(2)}) copy-start(bf16[576,1152]{1,0:T(8,128)(2,1)} %param.21) | copy-start | bytes 3981316
  6.4 1.7 collective-permute-start
  20.0 11.7 %copy-start.3 = (bf16[768,3,576]{0,2,1:T(8,128)(2,1)}, bf16[768,3,576]{0,2,1:T(8,128)(2,1)S(1)}, u32[]{:S(2)}) copy-start(bf16[768,3,576]{0,2,1:T(8,128)(2,1)S(1)} %add_convert_fusion) | copy-start | bytes 7962628
  34.7 9.6 %collective-permute-start.1 = (bf16[768,1152]{1,0:T(8,128)(2,1)}, bf16[768,1152]{1,0:T(8,128)(2,1)}, u32[]{:S(2)}, u32[]{:S(2)}) collective-permute-start(bf16[768,1152]{1,0:T(8,128)(2,1)} %convolution_convert_fusion.5), channel_id=1, source_target_pairs={{0,1},{1,0},{2,3},{3,2},{4,5},{5,4},{6,7},{7,6},{8,9},{9,8},{10,11... | collective-permute-start | bytes 5308424 | tf_op jit(solution)/shard_map/ppermute | solution.py:199
  44.3 23.3 %copy-start.48 = (bf16[768,1152]{1,0:T(8,128)(2,1)}, bf16[768,1152]{1,0:T(8,128)(2,1)S(1)}, u32[]{:S(2)}) copy-start(bf16[768,1152]{1,0:T(8,128)(2,1)S(1)} %get-tuple-element.83) | copy-start | bytes 5308420
  51.8 68.3 %copy-start.7 = (f32[768,1152]{1,0:T(8,128)}, f32[768,1152]{1,0:T(8,128)S(1)}, u32[]{:S(2)}) copy-start(f32[768,1152]{1,0:T(8,128)S(1)} %get-tuple-element.218) | copy-start | bytes 10616836
  74.5 32.6 %collective-permute-start.2 = (bf16[2,2,2,1,72,1152]{5,4,3,2,1,0:T(8,128)(2,1)}, bf16[2,2,2,1,72,1152]{5,4,3,2,1,0:T(8,128)(2,1)}, u32[]{:S(2)}, u32[]{:S(2)}) collective-permute-start(bf16[2,2,2,1,72,1152]{5,4,3,2,1,0:T(8,128)(2,1)} %constant_dynamic-slice_fusion.16), channel_id=1, source_target_pairs={{0,2},{2,0},{4,6},{6,4},{8,10},{10,8},{12,14},{14,12},{16,18},{18,... | collective-permute-start | bytes 3981320 | tf_op jit(solution)/shard_map/ppermute | solution.py:265
  77.3 31.1 %collective-permute-start.3 = (bf16[2,2,1,2,72,1152]{5,4,3,2,1,0:T(8,128)(2,1)S(1)}, bf16[2,2,1,2,72,1152]{5,4,3,2,1,0:T(8,128)(2,1)}, u32[]{:S(2)}, u32[]{:S(2)}) collective-permute-start(bf16[2,2,1,2,72,1152]{5,4,3,2,1,0:T(8,128)(2,1)S(1)} %constant_dynamic-slice_fusion.15), channel_id=1, source_target_pairs={{0,4},{2,6},{4,0},{6,2},{8,12},{10,14},{12,8},{14,10},{16,20},{18,... | collective-permute-start | bytes 3981320 | tf_op jit(solution)/shard_map/ppermute | solution.py:265
  99.6 16.7 %collective-permute-start.4 = (bf16[768,1152]{1,0:T(8,128)(2,1)S(1)}, bf16[768,1152]{1,0:T(8,128)(2,1)S(1)}, u32[]{:S(2)}, u32[]{:S(2)}) collective-permute-start(bf16[768,1152]{1,0:T(8,128)(2,1)S(1)} %convolution_convert_fusion.7), channel_id=1, source_target_pairs={{0,1},{1,0},{2,3},{3,2},{4,5},{5,4},{6,7},{7,6},{8,9},{9,8},{10,11... | collective-permute-start | bytes 5308424 | tf_op jit(solution)/shard_map/ppermute | solution.py:199
  117.9 16.6 %collective-permute-start.5 = (bf16[2,2,1,1,72,1152]{5,4,3,2,1,0:T(8,128)(2,1)}, bf16[2,2,1,1,72,1152]{5,4,3,2,1,0:T(8,128)(2,1)S(1)}, u32[]{:S(2)}, u32[]{:S(2)}) collective-permute-start(bf16[2,2,1,1,72,1152]{5,4,3,2,1,0:T(8,128)(2,1)} %get-tuple-element.88), channel_id=1, source_target_pairs={{0,4},{2,6},{4,0},{6,2},{8,12},{10,14},{12,8},{14,10},{16,20},{18,... | collective-permute-start | bytes 1990664 | tf_op jit(solution)/shard_map/ppermute | solution.py:265
  119.6 15.6 %collective-permute-start.6 = (bf16[2,2,1,1,72,1152]{5,4,3,2,1,0:T(8,128)(2,1)S(1)}, bf16[2,2,1,1,72,1152]{5,4,3,2,1,0:T(8,128)(2,1)S(1)}, u32[]{:S(2)}, u32[]{:S(2)}) collective-permute-start(bf16[2,2,1,1,72,1152]{5,4,3,2,1,0:T(8,128)(2,1)S(1)} %get-tuple-element.89), channel_id=1, source_target_pairs={{0,2},{2,0},{4,6},{6,4},{8,10},{10,8},{12,14},{14,12},{16,18},{18,... | collective-permute-start | bytes 1990664 | tf_op jit(solution)/shard_map/ppermute | solution.py:265
  125.4 9.7 %copy-start.30 = (bf16[2,2,1,2,72,1152]{5,4,3,2,1,0:T(8,128)(2,1)S(1)}, bf16[2,2,1,2,72,1152]{5,4,3,2,1,0:T(8,128)(2,1)}, u32[]{:S(2)}) copy-start(bf16[2,2,1,2,72,1152]{5,4,3,2,1,0:T(8,128)(2,1)} %copy-done.29) | copy-start | bytes 3981316
  125.4 11.3 %copy-start.28 = (bf16[2,2,2,1,72,1152]{5,4,3,2,1,0:T(8,128)(2,1)S(1)}, bf16[2,2,2,1,72,1152]{5,4,3,2,1,0:T(8,128)(2,1)}, u32[]{:S(2)}) copy-start(bf16[2,2,2,1,72,1152]{5,4,3,2,1,0:T(8,128)(2,1)} %copy-done.27) | copy-start | bytes 3981316
  135.4 29.5 %collective-permute-start.7 = (bf16[2,2,2,1,72,1152]{5,4,3,2,1,0:T(8,128)(2,1)}, bf16[2,2,2,1,72,1152]{5,4,3,2,1,0:T(8,128)(2,1)}, u32[]{:S(2)}, u32[]{:S(2)}) collective-permute-start(bf16[2,2,2,1,72,1152]{5,4,3,2,1,0:T(8,128)(2,1)} %constant_dynamic-slice_fusion.14), channel_id=1, source_target_pairs={{0,2},{2,0},{4,6},{6,4},{8,10},{10,8},{12,14},{14,12},{16,18},{18,... | collective-permute-start | bytes 3981320 | tf_op jit(solution)/shard_map/ppermute | solution.py:265
  136.3 29.2 %collective-permute-start.8 = (bf16[2,2,1,2,72,1152]{5,4,3,2,1,0:T(8,128)(2,1)}, bf16[2,2,1,2,72,1152]{5,4,3,2,1,0:T(8,128)(2,1)}, u32[]{:S(2)}, u32[]{:S(2)}) collective-permute-start(bf16[2,2,1,2,72,1152]{5,4,3,2,1,0:T(8,128)(2,1)} %constant_dynamic-slice_fusion.13), channel_id=1, source_target_pairs={{0,4},{2,6},{4,0},{6,2},{8,12},{10,14},{12,8},{14,10},{16,20},{18,... | collective-permute-start | bytes 3981320 | tf_op jit(solution)/shard_map/ppermute | solution.py:265
  138.0 27.5 %collective-permute-start.9 = (bf16[2,1,1,1,72,2304]{5,4,3,2,1,0:T(8,128)(2,1)}, bf16[2,1,1,1,72,2304]{5,4,3,2,1,0:T(8,128)(2,1)}, u32[]{:S(2)}, u32[]{:S(2)}) collective-permute-start(bf16[2,1,1,1,72,2304]{5,4,3,2,1,0:T(8,128)(2,1)} %fusion.82), channel_id=1, source_target_pairs={{0,8},{2,10},{4,12},{6,14},{8,0},{10,2},{12,4},{14,6},{16,24},{18,... | collective-permute-start | bytes 1990664 | tf_op jit(solution)/shard_map/ppermute | solution.py:265
  143.3 22.2 %copy-start.40 = (bf16[1152,1152]{1,0:T(8,128)(2,1)S(1)}, bf16[1152,1152]{1,0:T(8,128)(2,1)}, u32[]{:S(2)}) copy-start(bf16[1152,1152]{1,0:T(8,128)(2,1)} %copy-done.39) | copy-start | bytes 7962628
  173.7 13.8 %collective-permute-start.10 = (bf16[2,2,1,1,72,1152]{5,4,3,2,1,0:T(8,128)(2,1)S(1)}, bf16[2,2,1,1,72,1152]{5,4,3,2,1,0:T(8,128)(2,1)S(1)}, u32[]{:S(2)}, u32[]{:S(2)}) collective-permute-start(bf16[2,2,1,1,72,1152]{5,4,3,2,1,0:T(8,128)(2,1)S(1)} %constant_dynamic-slice_fusion.10), channel_id=1, source_target_pairs={{0,4},{2,6},{4,0},{6,2},{8,12},{10,14},{12,8},{14,10},{16,20},{18,... | collective-permute-start | bytes 1990664 | tf_op jit(solution)/shard_map/ppermute | solution.py:265
  174.6 13.8 %collective-permute-start.11 = (bf16[2,2,1,1,72,1152]{5,4,3,2,1,0:T(8,128)(2,1)S(1)}, bf16[2,2,1,1,72,1152]{5,4,3,2,1,0:T(8,128)(2,1)S(1)}, u32[]{:S(2)}, u32[]{:S(2)}) collective-permute-start(bf16[2,2,1,1,72,1152]{5,4,3,2,1,0:T(8,128)(2,1)S(1)} %constant_dynamic-slice_fusion.9), channel_id=1, source_target_pairs={{0,2},{2,0},{4,6},{6,4},{8,10},{10,8},{12,14},{14,12},{16,18},{18,... | collective-permute-start | bytes 1990664 | tf_op jit(solution)/shard_map/ppermute | solution.py:265
  176.2 14.4 %collective-permute-start.12 = (bf16[1,1,1,1,72,2304]{5,4,3,2,1,0:T(8,128)(2,1)S(1)}, bf16[1,1,1,1,72,2304]{5,4,3,2,1,0:T(8,128)(2,1)}, u32[]{:S(2)}, u32[]{:S(2)}) collective-permute-start(bf16[1,1,1,1,72,2304]{5,4,3,2,1,0:T(8,128)(2,1)S(1)} %constant_dynamic-slice_fusion.8), channel_id=1, source_target_pairs={{0,16},{2,18},{4,20},{6,22},{8,24},{10,26},{12,28},{14,30},{16,0},... | collective-permute-start | bytes 995336 | tf_op jit(solution)/shard_map/ppermute | solution.py:265
  211.8 12.3 %collective-permute-start.13 = (bf16[768,576]{0,1:T(8,128)(2,1)}, bf16[768,576]{0,1:T(8,128)(2,1)}, u32[]{:S(2)}, u32[]{:S(2)}) collective-permute-start(bf16[768,576]{0,1:T(8,128)(2,1)} %copy.48), channel_id=1, source_target_pairs={{0,1},{1,0},{2,3},{3,2},{4,5},{5,4},{6,7},{7,6},{8,9},{9,8},{10,11... | collective-permute-start | bytes 2654216 | tf_op jit(solution)/shard_map/ppermute | solution.py:199
  221.2 47.6 %collective-permute-start.18 = (bf16[2,2,2,1,72,1152]{5,4,3,2,1,0:T(8,128)(2,1)}, bf16[2,2,2,1,72,1152]{5,4,3,2,1,0:T(8,128)(2,1)}, u32[]{:S(2)}, u32[]{:S(2)}) collective-permute-start(bf16[2,2,2,1,72,1152]{5,4,3,2,1,0:T(8,128)(2,1)} %constant_dynamic-slice_fusion.7), channel_id=1, source_target_pairs={{0,2},{2,0},{4,6},{6,4},{8,10},{10,8},{12,14},{14,12},{16,18},{18,... | collective-permute-start | bytes 3981320 | tf_op jit(solution)/shard_map/ppermute | solution.py:265
  221.8 47.0 %collective-permute-start.19 = (bf16[2,2,1,2,72,1152]{5,4,3,2,1,0:T(8,128)(2,1)}, bf16[2,2,1,2,72,1152]{5,4,3,2,1,0:T(8,128)(2,1)}, u32[]{:S(2)}, u32[]{:S(2)}) collective-permute-start(bf16[2,2,1,2,72,1152]{5,4,3,2,1,0:T(8,128)(2,1)} %constant_dynamic-slice_fusion.6), channel_id=1, source_target_pairs={{0,4},{2,6},{4,0},{6,2},{8,12},{10,14},{12,8},{14,10},{16,20},{18,... | collective-permute-start | bytes 3981320 | tf_op jit(solution)/shard_map/ppermute | solution.py:265
  222.7 46.1 %collective-permute-start.20 = (bf16[2,1,1,1,72,2304]{5,4,3,2,1,0:T(8,128)(2,1)}, bf16[2,1,1,1,72,2304]{5,4,3,2,1,0:T(8,128)(2,1)}, u32[]{:S(2)}, u32[]{:S(2)}) collective-permute-start(bf16[2,1,1,1,72,2304]{5,4,3,2,1,0:T(8,128)(2,1)} %fusion.80), channel_id=1, source_target_pairs={{0,8},{2,10},{4,12},{6,14},{8,0},{10,2},{12,4},{14,6},{16,24},{18,... | collective-permute-start | bytes 1990664 | tf_op jit(solution)/shard_map/ppermute | solution.py:265
  230.2 11.0 %copy-start.16 = (bf16[768,1152]{1,0:T(8,128)(2,1)S(1)}, bf16[768,1152]{1,0:T(8,128)(2,1)}, u32[]{:S(2)}) copy-start(bf16[768,1152]{1,0:T(8,128)(2,1)} %copy-done.15) | copy-start | bytes 5308420
  230.2 12.1 %copy-start.12 = (f32[768,1152]{1,0:T(8,128)S(1)}, f32[768,1152]{1,0:T(8,128)}, u32[]{:S(2)}) copy-start(f32[768,1152]{1,0:T(8,128)} %get-tuple-element.220) | copy-start | bytes 10616836
  238.9 22.6 %collective-permute-start.14 = (bf16[768,1152]{1,0:T(8,128)(2,1)}, bf16[768,1152]{1,0:T(8,128)(2,1)}, u32[]{:S(2)}, u32[]{:S(2)}) collective-permute-start(bf16[768,1152]{1,0:T(8,128)(2,1)} %convolution_convert_fusion.6), channel_id=1, source_target_pairs={{0,1},{1,0},{2,3},{3,2},{4,5},{5,4},{6,7},{7,6},{8,9},{9,8},{10,11... | collective-permute-start | bytes 5308424 | tf_op jit(solution)/shard_map/ppermute | solution.py:199
  240.7 11.3 %copy-start.14 = (f32[768,1152]{1,0:T(8,128)S(1)}, f32[768,1152]{1,0:T(8,128)}, u32[]{:S(2)}) copy-start(f32[768,1152]{1,0:T(8,128)} %get-tuple-element.209) | copy-start | bytes 10616836
  240.7 4.0 %collective-permute-start.15 = (bf16[768]{0:T(1024)(128)(2,1)S(1)}, bf16[768]{0:T(1024)(128)(2,1)S(1)}, u32[]{:S(2)}, u32[]{:S(2)}) collective-permute-start(bf16[768]{0:T(1024)(128)(2,1)S(1)} %get-tuple-element.119), channel_id=1, source_target_pairs={{0,1},{1,0},{2,3},{3,2},{4,5},{5,4},{6,7},{7,6},{8,9},{9,8},{10,11... | collective-permute-start | bytes 4616 | tf_op jit(solution)/shard_map/ppermute | solution.py:199
  244.8 1.2 collective-permute-start.16
  245.9 5.1 %collective-permute-start.25 = (bf16[1,20,576]{2,1,0:T(8,128)(2,1)S(1)}, bf16[1,20,576]{2,1,0:T(8,128)(2,1)S(1)}, u32[]{:S(2)}, u32[]{:S(2)}) collective-permute-start(bf16[1,20,576]{2,1,0:T(8,128)(2,1)S(1)} %maximum_bitcast_fusion.1), channel_id=1, source_target_pairs={{0,16},{2,18},{4,20},{6,22},{8,24},{10,26},{12,28},{14,30},{16,0},... | collective-permute-start | bytes 69128 | tf_op jit(solution)/shard_map/ppermute | solution.py:233
  251.7 8.9 %collective-permute-start.26 = (bf16[2,20,576]{2,1,0:T(8,128)(2,1)}, bf16[2,20,576]{2,1,0:T(8,128)(2,1)}, u32[]{:S(2)}, u32[]{:S(2)}) collective-permute-start(bf16[2,20,576]{2,1,0:T(8,128)(2,1)} %pad_maximum_fusion.10), channel_id=1, source_target_pairs={{0,8},{2,10},{4,12},{6,14},{8,0},{10,2},{12,4},{14,6},{16,24},{18,... | collective-permute-start | bytes 138248 | tf_op jit(solution)/shard_map/ppermute | solution.py:233
  266.8 21.1 %slice-start = ((s8[7962624]{0:T(1024)(128)(4,1)}), s8[4194304]{0:T(1024)(128)(4,1)S(1)}, s32[]{:S(2)}) async-start(s8[7962624]{0:T(1024)(128)(4,1)} %bitcast.182), calls=%async_computation | async-start | bytes 8388608
  270.6 17.2 %slice-start.1 = ((s8[7962624]{0:T(1024)(128)(4,1)}), s8[3768320]{0:T(1024)(128)(4,1)S(1)}, s32[]{:S(2)}) async-start(s8[7962624]{0:T(1024)(128)(4,1)} %bitcast.182), calls=%async_computation.1 | async-start | bytes 7536640
  272.6 15.3 %copy-start.65 = (bf16[2,8,576]{2,1,0:T(8,128)(2,1)S(1)}, bf16[2,8,576]{2,1,0:T(8,128)(2,1)}, u32[]{:S(2)}) copy-start(bf16[2,8,576]{2,1,0:T(8,128)(2,1)} %maximum_convert_fusion.1) | copy-start | bytes 55300
  274.3 5.7 %collective-permute-start.23 = (bf16[1,64,576]{2,1,0:T(8,128)(2,1)S(1)}, bf16[1,64,576]{2,1,0:T(8,128)(2,1)S(1)}, u32[]{:S(2)}, u32[]{:S(2)}) collective-permute-start(bf16[1,64,576]{2,1,0:T(8,128)(2,1)S(1)} %maximum_bitcast_fusion), channel_id=1, source_target_pairs={{0,16},{2,18},{4,20},{6,22},{8,24},{10,26},{12,28},{14,30},{16,0},... | collective-permute-start | bytes 221192 | tf_op jit(solution)/shard_map/ppermute | solution.py:233
  276.7 18.9 %collective-permute-start.21 = (bf16[2,2,1,1,72,1152]{5,4,3,2,1,0:T(8,128)(2,1)S(1)}, bf16[2,2,1,1,72,1152]{5,4,3,2,1,0:T(8,128)(2,1)S(1)}, u32[]{:S(2)}, u32[]{:S(2)}) collective-permute-start(bf16[2,2,1,1,72,1152]{5,4,3,2,1,0:T(8,128)(2,1)S(1)} %constant_dynamic-slice_fusion.4), channel_id=1, source_target_pairs={{0,4},{2,6},{4,0},{6,2},{8,12},{10,14},{12,8},{14,10},{16,20},{18,... | collective-permute-start | bytes 1990664 | tf_op jit(solution)/shard_map/ppermute | solution.py:265
  277.7 17.9 %collective-permute-start.22 = (bf16[2,2,1,1,72,1152]{5,4,3,2,1,0:T(8,128)(2,1)S(1)}, bf16[2,2,1,1,72,1152]{5,4,3,2,1,0:T(8,128)(2,1)S(1)}, u32[]{:S(2)}, u32[]{:S(2)}) collective-permute-start(bf16[2,2,1,1,72,1152]{5,4,3,2,1,0:T(8,128)(2,1)S(1)} %constant_dynamic-slice_fusion.3), channel_id=1, source_target_pairs={{0,2},{2,0},{4,6},{6,4},{8,10},{10,8},{12,14},{14,12},{16,18},{18,... | collective-permute-start | bytes 1990664 | tf_op jit(solution)/shard_map/ppermute | solution.py:265
  279.1 17.0 %collective-permute-start.27 = (bf16[1,1,1,1,72,2304]{5,4,3,2,1,0:T(8,128)(2,1)S(1)}, bf16[1,1,1,1,72,2304]{5,4,3,2,1,0:T(8,128)(2,1)S(1)}, u32[]{:S(2)}, u32[]{:S(2)}) collective-permute-start(bf16[1,1,1,1,72,2304]{5,4,3,2,1,0:T(8,128)(2,1)S(1)} %constant_dynamic-slice_fusion.2), channel_id=1, source_target_pairs={{0,16},{2,18},{4,20},{6,22},{8,24},{10,26},{12,28},{14,30},{16,0},... | collective-permute-start | bytes 995336 | tf_op jit(solution)/shard_map/ppermute | solution.py:265
  280.0 15.5 %collective-permute-start.24 = (bf16[2,64,576]{2,1,0:T(8,128)(2,1)S(1)}, bf16[2,64,576]{2,1,0:T(8,128)(2,1)S(1)}, u32[]{:S(2)}, u32[]{:S(2)}) collective-permute-start(bf16[2,64,576]{2,1,0:T(8,128)(2,1)S(1)} %pad_maximum_fusion.8), channel_id=1, source_target_pairs={{0,8},{2,10},{4,12},{6,14},{8,0},{10,2},{12,4},{14,6},{16,24},{18,... | collective-permute-start | bytes 442376 | tf_op jit(solution)/shard_map/ppermute | solution.py:233
  289.0 9.4 %collective-permute-start.17 = (bf16[8,1152]{1,0:T(8,128)(2,1)S(1)}, bf16[8,1152]{1,0:T(8,128)(2,1)S(1)}, u32[]{:S(2)}, u32[]{:S(2)}) collective-permute-start(bf16[8,1152]{1,0:T(8,128)(2,1)S(1)} %fusion.16), channel_id=1, source_target_pairs={{0,1},{1,0},{2,3},{3,2},{4,5},{5,4},{6,7},{7,6},{8,9},{9,8},{10,11... | collective-permute-start | bytes 55304 | tf_op jit(solution)/shard_map/ppermute | solution.py:199
  296.1 6.5 %collective-permute-start.31 = (bf16[4,20,576]{2,1,0:T(8,128)(2,1)S(1)}, bf16[4,20,576]{2,1,0:T(8,128)(2,1)S(1)}, u32[]{:S(2)}, u32[]{:S(2)}) collective-permute-start(bf16[4,20,576]{2,1,0:T(8,128)(2,1)S(1)} %pad_maximum_fusion.9), channel_id=1, source_target_pairs={{0,4},{2,6},{4,0},{6,2},{8,12},{10,14},{12,8},{14,10},{16,20},{18,... | collective-permute-start | bytes 276488 | tf_op jit(solution)/shard_map/ppermute | solution.py:233
  298.3 8.3 %collective-permute-start.29 = (bf16[4,64,576]{2,1,0:T(8,128)(2,1)S(1)}, bf16[4,64,576]{2,1,0:T(8,128)(2,1)S(1)}, u32[]{:S(2)}, u32[]{:S(2)}) collective-permute-start(bf16[4,64,576]{2,1,0:T(8,128)(2,1)S(1)} %pad_maximum_fusion.6), channel_id=1, source_target_pairs={{0,4},{2,6},{4,0},{6,2},{8,12},{10,14},{12,8},{14,10},{16,20},{18,... | collective-permute-start | bytes 884744 | tf_op jit(solution)/shard_map/ppermute | solution.py:233
  299.1 28.0 %collective-permute-start.28 = (bf16[2,1,1,1,72,2304]{5,4,3,2,1,0:T(8,128)(2,1)S(1)}, bf16[2,1,1,1,72,2304]{5,4,3,2,1,0:T(8,128)(2,1)S(1)}, u32[]{:S(2)}, u32[]{:S(2)}) collective-permute-start(bf16[2,1,1,1,72,2304]{5,4,3,2,1,0:T(8,128)(2,1)S(1)} %fusion.77), channel_id=1, source_target_pairs={{0,8},{2,10},{4,12},{6,14},{8,0},{10,2},{12,4},{14,6},{16,24},{18,... | collective-permute-start | bytes 1990664 | tf_op jit(solution)/shard_map/ppermute | solution.py:265
  302.6 10.7 %collective-permute-start.32 = (bf16[8,20,576]{2,1,0:T(8,128)(2,1)S(1)}, bf16[8,20,576]{2,1,0:T(8,128)(2,1)S(1)}, u32[]{:S(2)}, u32[]{:S(2)}) collective-permute-start(bf16[8,20,576]{2,1,0:T(8,128)(2,1)S(1)} %pad_maximum_fusion.7), channel_id=1, source_target_pairs={{0,2},{2,0},{4,6},{6,4},{8,10},{10,8},{12,14},{14,12},{16,18},{18,... | collective-permute-start | bytes 552968 | tf_op jit(solution)/shard_map/ppermute | solution.py:233
  306.7 20.1 %collective-permute-start.30 = (bf16[8,64,576]{2,1,0:T(8,128)(2,1)S(1)}, bf16[8,64,576]{2,1,0:T(8,128)(2,1)S(1)}, u32[]{:S(2)}, u32[]{:S(2)}) collective-permute-start(bf16[8,64,576]{2,1,0:T(8,128)(2,1)S(1)} %pad_maximum_fusion.3), channel_id=1, source_target_pairs={{0,2},{2,0},{4,6},{6,4},{8,10},{10,8},{12,14},{14,12},{16,18},{18,... | collective-permute-start | bytes 1769480 | tf_op jit(solution)/shard_map/ppermute | solution.py:233
  330.2 16.8 %collective-permute-start.33 = (bf16[1,1,1,1,72,2304]{5,4,3,2,1,0:T(8,128)(2,1)}, bf16[1,1,1,1,72,2304]{5,4,3,2,1,0:T(8,128)(2,1)}, u32[]{:S(2)}, u32[]{:S(2)}) collective-permute-start(bf16[1,1,1,1,72,2304]{5,4,3,2,1,0:T(8,128)(2,1)} %constant_dynamic-slice_fusion.1), channel_id=1, source_target_pairs={{0,16},{2,18},{4,20},{6,22},{8,24},{10,26},{12,28},{14,30},{16,0},... | collective-permute-start | bytes 995336 | tf_op jit(solution)/shard_map/ppermute | solution.py:265
  333.2 16.8 %copy-start.1 = (bf16[576,1152]{1,0:T(8,128)(2,1)S(1)}, bf16[576,1152]{1,0:T(8,128)(2,1)}, u32[]{:S(2)}) copy-start(bf16[576,1152]{1,0:T(8,128)(2,1)} %param.21) | copy-start | bytes 3981316
  (70 other events, 253.6 us)
